TPU v7x, 512 devices: a whole 4x4x16 slice. The times are simulated.
512 devices in a mesh: seq: 64 (over z, x), head: 8 (over y, core).
Axes of the slice: x: 4, y: 4, z: 16, core: 2. Of those that a mesh axis runs over, the one named last changes fastest.
Arguments:
- queries: bfloat16 [16384, 8192], P(('seq', 'head')), may hold values from -6 to 6
- key_vectors: bfloat16 [16384, 8192], P(('seq', 'head')), may hold values from -6 to 6
- value_vectors: bfloat16 [16384, 8192], P(('seq', 'head')), may hold values from -6 to 6
- out_grad: bfloat16 [16384, 8192], P(('seq', 'head')), may hold values from -6 to 6
Outputs:
- query_grad: bfloat16 [16384, 8192], P(('seq', 'head'))
- key_grad: bfloat16 [16384, 8192], P(('seq', 'head'))
- value_grad: bfloat16 [16384, 8192], P(('seq', 'head'))
All inputs are finite; a program needn't handle non-finite values.
Results may differ from a plain program's by a relative error of at most 0.005.
Values may be sent and summed in bfloat16 or wider, within the bound.
No kernel may reach another device: no remote copies, remote signals or barrier semaphores. Data moves between devices by JAX's collectives and lax.ppermute only.
A program may use at most 192 MiB of HBM per device.

v0:
```python
import jax
import jax.numpy as jnp
from jax import lax
from jax.sharding import PartitionSpec as P

HEAD_DIM = 128


def carried_in(value, axis, combine, identity, reverse):
    peers, here = (lax.axis_size(axis), lax.axis_index(axis))
    everything = lax.all_gather(value, axis)
    start = jnp.broadcast_to(jnp.asarray(identity, value.dtype), value.shape)

    def turn(k, before):
        at = peers - 1 - k if reverse else k
        reached = at > here if reverse else at < here
        new = combine(before, everything[at])
        return jnp.where(reached, new, before)

    return lax.fori_loop(0, peers, turn, start)


def combine_sum(earlier, later):
    return jax.tree.map(jnp.add, earlier, later)


def local(queries, key_vectors, value_vectors, out_grad):
    f32 = jnp.float32
    hi = lax.Precision.HIGHEST
    groups = lax.axis_size("head")
    rows = queries.shape[0] * groups
    width = queries.shape[1] // groups
    heads = width // HEAD_DIM
    q_loc, k_loc, v_loc, g_loc = (
        lax.all_to_all(queries, "head", split_axis=1, concat_axis=0, tiled=True),
        lax.all_to_all(key_vectors, "head", split_axis=1, concat_axis=0, tiled=True),
        lax.all_to_all(value_vectors, "head", split_axis=1, concat_axis=0, tiled=True),
        lax.all_to_all(out_grad, "head", split_axis=1, concat_axis=0, tiled=True),
    )
    start = (lax.axis_index("seq") * rows).astype(f32)
    position = jnp.arange(rows, dtype=f32) + start
    factor = lax.rsqrt(HEAD_DIM * (position + 1.0))
    scaled = (g_loc.astype(f32) * factor[:, None]).astype(jnp.bfloat16)

    def head_major(x):
        return jnp.transpose(x.reshape(rows, heads, HEAD_DIM), (1, 0, 2))

    qh = head_major(q_loc)
    kh = head_major(k_loc)
    vh = head_major(v_loc)
    gh = head_major(scaled)
    kv_sum = jnp.einsum("htd,hte->hde", kh, vh, preferred_element_type=f32)
    qg_sum = jnp.einsum("htd,hte->hde", qh, gh, preferred_element_type=f32)
    zero_state = jnp.zeros((heads, HEAD_DIM, HEAD_DIM), f32)
    before = carried_in(kv_sum, "seq", combine_sum, zero_state, False)
    after = carried_in(qg_sum, "seq", combine_sum, zero_state, True)
    index = jnp.arange(rows, dtype=jnp.int32)
    keep = index[:, None] >= index[None, :]
    inner = jnp.where(
        keep[None], jnp.einsum("hte,hse->hts", gh, vh, preferred_element_type=f32), 0.0
    ).astype(jnp.bfloat16)
    pairs = jnp.where(
        keep[None], jnp.einsum("htd,hsd->hts", qh, kh, preferred_element_type=f32), 0.0
    ).astype(jnp.bfloat16)
    dq = jnp.einsum("hts,hsd->htd", inner, kh, preferred_element_type=f32) + jnp.einsum(
        "hte,hde->htd", gh.astype(f32), before, precision=hi
    )
    dk = jnp.einsum("hts,htd->hsd", inner, qh, preferred_element_type=f32) + jnp.einsum(
        "hse,hde->hsd", vh.astype(f32), after, precision=hi
    )
    dv = jnp.einsum("hts,hte->hse", pairs, gh, preferred_element_type=f32) + jnp.einsum(
        "hsd,hde->hse", kh.astype(f32), after, precision=hi
    )

    def token_major(x):
        return jnp.transpose(x.astype(jnp.bfloat16), (1, 0, 2)).reshape(rows, width)

    dq_loc = token_major(dq)
    dk_loc = token_major(dk)
    dv_loc = token_major(dv)
    query_grad, key_grad, value_grad = (
        lax.all_to_all(dq_loc, "head", split_axis=0, concat_axis=1, tiled=True),
        lax.all_to_all(dk_loc, "head", split_axis=0, concat_axis=1, tiled=True),
        lax.all_to_all(dv_loc, "head", split_axis=0, concat_axis=1, tiled=True),
    )
    return (query_grad, key_grad, value_grad)


def solution(mesh):
    placed = (
        P(("seq", "head"), None),
        P(("seq", "head"), None),
        P(("seq", "head"), None),
        P(("seq", "head"), None),
    )
    return jax.shard_map(
        local,
        mesh=mesh,
        in_specs=placed,
        out_specs=(P(("seq", "head"), None), P(("seq", "head"), None), P(("seq", "head"), None)),
        check_vma=False,
    )
```

profile of v0, /device:TPU:1, one launch (start us, length us, event | category | flops | bytes accessed | tf_op | source)
XLA Modules:
  0.0 733.2 jit_solution(7795061028266321221)
XLA Ops:
  7.2 1.9 copy.158
  9.1 10.2 %all-to-all-start = ((bf16[32,8,1024]{2,0,1:T(8,128)(2,1)}), bf16[32,8,1024]{2,0,1:T(8,128)(2,1)S(1)}, u32[]{:S(2)}, u32[]{:S(2)}) async-start(bf16[32,8,1024]{2,0,1:T(8,128)(2,1)} %bitcast.100), calls=%async_computation | async-start | bytes 1048576 | tf_op jit(solution)/shard_map/all_to_all | solution.py:38
  20.2 8.5 %all-to-all-done = bf16[32,8,1024]{2,0,1:T(8,128)(2,1)S(1)} async-done(((bf16[32,8,1024]{2,0,1:T(8,128)(2,1)}), bf16[32,8,1024]{2,0,1:T(8,128)(2,1)S(1)}, u32[]{:S(2)}, u32[]{:S(2)}) %all-to-all-start) | async-done | bytes 524320 | tf_op jit(solution)/shard_map/all_to_all | solution.py:38
  28.7 4.4 all-to-all-start.4
  33.4 9.0 %all-to-all-done.4 = bf16[32,8,1024]{2,0,1:T(8,128)(2,1)S(1)} async-done(((bf16[32,8,1024]{2,0,1:T(8,128)(2,1)}), bf16[32,8,1024]{2,0,1:T(8,128)(2,1)S(1)}, u32[]{:S(2)}, u32[]{:S(2)}) %all-to-all-start.4) | async-done | bytes 524320 | tf_op jit(solution)/shard_map/all_to_all | solution.py:35
  45.1 4.4 all-to-all-start.2
  50.3 8.5 %all-to-all-done.2 = bf16[32,8,1024]{2,0,1:T(8,128)(2,1)S(1)} async-done(((bf16[32,8,1024]{2,0,1:T(8,128)(2,1)}), bf16[32,8,1024]{2,0,1:T(8,128)(2,1)S(1)}, u32[]{:S(2)}, u32[]{:S(2)}) %all-to-all-start.2) | async-done | bytes 524320 | tf_op jit(solution)/shard_map/all_to_all | solution.py:36
  58.9 4.4 all-to-all-start.1
  63.4 9.3 %all-to-all-done.1 = bf16[32,8,1024]{2,0,1:T(8,128)(2,1)S(1)} async-done(((bf16[32,8,1024]{2,0,1:T(8,128)(2,1)}), bf16[32,8,1024]{2,0,1:T(8,128)(2,1)S(1)}, u32[]{:S(2)}, u32[]{:S(2)}) %all-to-all-start.1) | async-done | bytes 524320 | tf_op jit(solution)/shard_map/all_to_all | solution.py:37
  75.4 1.5 convolution_bitcast_fusion.2
  76.9 258.3 %all-gather.7.cloned.1.call-done = f32[512,128,128]{2,1,0:T(8,128)} async-done(((f32[8,128,128]{2,1,0:T(8,128)}), f32[512,128,128]{2,1,0:T(8,128)}) %all-gather.7.cloned.1.call-update) | async-done | bytes 33554448 | tf_op jit(solution)/shard_map/all_gather | solution.py:11
  335.2 80.6 %while.31 = (s32[]{:T(128)}, f32[8,128,128]{2,1,0:T(8,128)S(1)}, s32[]{:T(128)}, f32[64,8,128,128]{3,2,1,0:T(8,128)}, s32[]{:T(128)}, /*index=5*/s32[]{:T(128)}, s32[]{:T(128)}, s32[]{:T(128)}) while((s32[]{:T(128)}, f32[8,128,128]{2,1,0:T(8,128)S(1)}, s32[]{:T(128)}, f32[64,8,128,128]{3,2,1,0:T(8,128)}, s32[]{:T(128)}, ...), condition=%wide.region_3.4_spmd.clone, body=%wide.region_2.3_spmd.clone.sunk | while | flops 393224 | bytes 1573019 | solution.py:20
  356.6 1.2 add_select_fusion.5
  359.1 1.2 add_select_fusion.5
  360.4 1.2 add_select_fusion.5
  362.9 1.2 add_select_fusion.5
  364.2 1.2 add_select_fusion.5
  365.5 1.2 add_select_fusion.5
  366.7 1.2 add_select_fusion.5
  368.0 1.2 add_select_fusion.5
  370.5 1.2 add_select_fusion.5
  373.0 1.2 add_select_fusion.5
  374.3 1.2 add_select_fusion.5
  375.6 1.2 add_select_fusion.5
  378.1 1.2 add_select_fusion.5
  383.1 1.2 add_select_fusion.5
  386.9 1.2 add_select_fusion.5
  388.2 1.2 add_select_fusion.5
  389.4 1.2 add_select_fusion.5
  390.7 1.2 add_select_fusion.5
  392.0 1.2 add_select_fusion.5
  393.3 1.2 add_select_fusion.5
  397.0 1.2 add_select_fusion.5
  400.8 1.2 add_select_fusion.5
  403.3 1.2 add_select_fusion.5
  415.9 1.6 convolution_bitcast_fusion
  417.5 2.8 fusion.4
  420.2 1.4 copy.82
  422.6 5.9 all-to-all-start.6
  428.5 3.1 fusion.20
  433.5 4.4 all-to-all-done.6
  437.9 4.4 all-to-all-start.5
  442.3 186.0 %all-gather.5.cloned.1.call-done = f32[512,128,128]{2,1,0:T(8,128)} async-done(((f32[8,128,128]{2,1,0:T(8,128)}), f32[512,128,128]{2,1,0:T(8,128)}) %all-gather.5.cloned.1.call-update) | async-done | bytes 33554448 | tf_op jit(solution)/shard_map/all_gather | solution.py:11
  628.3 80.1 %while.30 = (s32[]{:T(128)}, f32[8,128,128]{2,1,0:T(8,128)S(1)}, s32[]{:T(128)}, f32[64,8,128,128]{3,2,1,0:T(8,128)}, s32[]{:T(128)}, /*index=5*/s32[]{:T(128)}) while((s32[]{:T(128)}, f32[8,128,128]{2,1,0:T(8,128)S(1)}, s32[]{:T(128)}, f32[64,8,128,128]{3,2,1,0:T(8,128)}, s32[]{:T(128)}, /*index=5*/s32[]{:T(128)}) %tuple.84), condition=%wide.region_1.2_spmd.clone, body=%wide.region_0.1_spmd.clone.sunk | while | flops 393220 | bytes 1572957 | solution.py:20
  628.3 1.3 add_select_fusion.4
  710.5 5.7 all-to-all-start.3
  716.1 1.9 copy.98
  718.8 6.6 all-to-all-done.3
  (147 shorter events, 141.7 us)
Async XLA Ops:
  7.2 12.2 %copy-start.3 = (bf16[32,8192]{1,0:T(8,128)(2,1)S(1)}, bf16[32,8192]{1,0:T(8,128)(2,1)}, u32[]{:S(2)}) copy-start(bf16[32,8192]{1,0:T(8,128)(2,1)} %param.8) | copy-start | bytes 1572868
  9.1 19.6 %all-to-all-start = ((bf16[32,8,1024]{2,0,1:T(8,128)(2,1)}), bf16[32,8,1024]{2,0,1:T(8,128)(2,1)S(1)}, u32[]{:S(2)}, u32[]{:S(2)}) async-start(bf16[32,8,1024]{2,0,1:T(8,128)(2,1)} %bitcast.100), calls=%async_computation | async-start | bytes 1048576 | tf_op jit(solution)/shard_map/all_to_all | solution.py:38
  28.7 13.7 %all-to-all-start.4 = ((bf16[32,8,1024]{2,0,1:T(8,128)(2,1)}), bf16[32,8,1024]{2,0,1:T(8,128)(2,1)S(1)}, u32[]{:S(2)}, u32[]{:S(2)}) async-start(bf16[32,8,1024]{2,0,1:T(8,128)(2,1)} %bitcast.97), calls=%async_computation.4 | async-start | bytes 1048576 | tf_op jit(solution)/shard_map/all_to_all | solution.py:35
  33.1 302.2 %all-gather.7.cloned.1.call-start = ((), (), s32[]{:S(2)}) async-start(), calls=%async_computation.8 | async-start | bytes 34078720 | tf_op jit(solution)/shard_map/all_gather | solution.py:11
  42.6 1.7 copy-start.4
  43.3 6.2 copy-start.5
  45.1 13.7 %all-to-all-start.2 = ((bf16[32,8,1024]{2,0,1:T(8,128)(2,1)}), bf16[32,8,1024]{2,0,1:T(8,128)(2,1)S(1)}, u32[]{:S(2)}, u32[]{:S(2)}) async-start(bf16[32,8,1024]{2,0,1:T(8,128)(2,1)} %bitcast.98), calls=%async_computation.2 | async-start | bytes 1048576 | tf_op jit(solution)/shard_map/all_to_all | solution.py:36
  58.9 13.7 %all-to-all-start.1 = ((bf16[32,8,1024]{2,0,1:T(8,128)(2,1)}), bf16[32,8,1024]{2,0,1:T(8,128)(2,1)S(1)}, u32[]{:S(2)}, u32[]{:S(2)}) async-start(bf16[32,8,1024]{2,0,1:T(8,128)(2,1)} %bitcast.99), calls=%async_computation.1 | async-start | bytes 1048576 | tf_op jit(solution)/shard_map/all_to_all | solution.py:37
  63.2 565.1 %all-gather.5.cloned.1.call-start = ((), (), s32[]{:S(2)}) async-start(), calls=%async_computation.7 | async-start | bytes 34078720 | tf_op jit(solution)/shard_map/all_gather | solution.py:11
  74.4 1.0 copy-start.1
  422.6 15.3 %all-to-all-start.6 = ((bf16[8,32,1024]{2,1,0:T(8,128)(2,1)}), bf16[8,32,1024]{2,1,0:T(8,128)(2,1)}, u32[]{:S(2)}, u32[]{:S(2)}) async-start(bf16[8,32,1024]{2,1,0:T(8,128)(2,1)} %all_to_all.107), calls=%async_computation.6 | async-start | bytes 1048576 | tf_op jit(solution)/shard_map/all_to_all | solution.py:84
  428.5 3.1 copy-start
  437.9 272.5 %all-to-all-start.5 = ((bf16[8,32,1024]{2,1,0:T(8,128)(2,1)}), bf16[8,32,1024]{2,1,0:T(8,128)(2,1)S(1)}, u32[]{:S(2)}, u32[]{:S(2)}) async-start(bf16[8,32,1024]{2,1,0:T(8,128)(2,1)} %all_to_all.103), calls=%async_computation.5 | async-start | bytes 1048576 | tf_op jit(solution)/shard_map/all_to_all | solution.py:83
  628.3 80.1 %copy-start.2 = (f32[8,256,128]{2,1,0:T(8,128)S(1)}, f32[8,256,128]{2,1,0:T(8,128)}, u32[]{:S(2)}) copy-start(f32[8,256,128]{2,1,0:T(8,128)} %fusion.20) | copy-start | bytes 3145732
  710.5 15.0 %all-to-all-start.3 = ((bf16[8,32,1024]{2,1,0:T(8,128)(2,1)}), bf16[8,32,1024]{2,1,0:T(8,128)(2,1)S(1)}, u32[]{:S(2)}, u32[]{:S(2)}) async-start(bf16[8,32,1024]{2,1,0:T(8,128)(2,1)} %all_to_all.96), calls=%async_computation.3 | async-start | bytes 1048576 | tf_op jit(solution)/shard_map/all_to_all | solution.py:82
Sparse Core Ops, SparseCore 0:
  44.4 290.7 all-gather.6
  338.8 289.5 all-gather.4
where the time goes:
time: 740 us; the launch traced here: 733 us
  waiting for transfers between devices  491 us (66%)
  other arithmetic  158 us (21%)
  starting transfers between devices  39.2 us (5%)
  local copies, waits for them, and re-layouts  15.6 us (2%)
  between operations  14.2 us (2%)
  matrix products  12 us (2%)
    all_gather x2, waiting for transfers between devices, carried_in(): everything = lax.all_gather(value, axis)  444 us
    select_n x128, other arithmetic, turn(): return jnp.where(reached, new, before)  157 us
  transfers between devices with their start and end apart: 9, of which 8 were waited for; matrix products, arithmetic and copies ran while one was open for 24% of the time, Pallas kernels for 0%

commit v1 on v0

v1 whole, which is shorter than its diff:
```python
import functools

import jax
import jax.numpy as jnp
from jax import lax
from jax.experimental import pallas as pl
from jax.experimental.pallas import tpu as pltpu
from jax.sharding import Mesh, PartitionSpec as P

HEAD_DIM = 128
ROWS = 32
CHUNK = 256
AXES = ("zh", "zl", "x", "y", "c")
GROUP = ("zl", "x", "y", "c")
F32 = jnp.float32
BF16 = jnp.bfloat16


def dot(a, b, ca, cb):
    return lax.dot_general(a, b, (((ca,), (cb,)), ((), ())), preferred_element_type=F32)


def params(*names):
    return pltpu.CompilerParams(
        dimension_semantics=("arbitrary",) * len(names), vmem_limit_bytes=48 * 1024 * 1024
    )


def split(x):
    high = x.astype(BF16)
    return high, (x - high.astype(F32)).astype(BF16)


def pack_kernel(q_ref, k_ref, v_ref, g_ref, o_ref):
    for a, ref in enumerate((q_ref, k_ref, v_ref, g_ref)):
        for j in range(o_ref.shape[0]):
            o_ref[j, a] = ref[:, j * HEAD_DIM : (j + 1) * HEAD_DIM]


def pack(q, k, v, g):
    rows, width = q.shape
    heads = width // HEAD_DIM
    step = 16
    return pl.pallas_call(
        pack_kernel,
        grid=(heads // step,),
        in_specs=[pl.BlockSpec((rows, step * HEAD_DIM), lambda i: (0, i))] * 4,
        out_specs=pl.BlockSpec((step, 4, rows, HEAD_DIM), lambda i: (i, 0, 0, 0)),
        out_shape=jax.ShapeDtypeStruct((heads, 4, rows, HEAD_DIM), q.dtype),
        compiler_params=params("i"),
        name="pack",
    )(q, k, v, g)


def unpack_kernel(x_ref, *o_refs):
    for a, ref in enumerate(o_refs):
        for j in range(x_ref.shape[0]):
            ref[:, j * HEAD_DIM : (j + 1) * HEAD_DIM] = x_ref[j, a]


def unpack(x):
    heads, n, rows, _ = x.shape
    step = 16
    return pl.pallas_call(
        unpack_kernel,
        grid=(heads // step,),
        in_specs=[pl.BlockSpec((step, n, rows, HEAD_DIM), lambda i: (i, 0, 0, 0))],
        out_specs=[pl.BlockSpec((rows, step * HEAD_DIM), lambda i: (0, i))] * n,
        out_shape=[jax.ShapeDtypeStruct((rows, heads * HEAD_DIM), x.dtype)] * n,
        compiler_params=params("i"),
        name="unpack",
    )(x)


def part(x_ref, a):
    return x_ref[:, a].reshape(CHUNK, HEAD_DIM)


def scaled_of(x_ref, me_ref, chunks):
    first = me_ref[0] * (chunks * CHUNK) + pl.program_id(0) * CHUNK
    place = lax.broadcasted_iota(jnp.int32, (CHUNK, HEAD_DIM), 0) + first
    factor = lax.rsqrt(HEAD_DIM * (place.astype(F32) + 1.0))
    return (part(x_ref, 3).astype(F32) * factor).astype(BF16)


def sums_kernel(me_ref, x_ref, slots_ref, pre_ref, suf_ref, kv_ref):
    i = pl.program_id(0)
    chunks = pl.num_programs(0)

    @pl.when(i == 0)
    def _():
        kv_ref[...] = jnp.zeros_like(kv_ref)

    g = scaled_of(x_ref, me_ref, chunks)
    pre_ref[i] = kv_ref[...]
    kv_ref[...] += dot(part(x_ref, 1), part(x_ref, 2), 0, 0)
    suf_ref[i] = dot(part(x_ref, 0), g, 0, 0)

    @pl.when(i == chunks - 1)
    def _():
        total = jnp.zeros((HEAD_DIM, HEAD_DIM), F32)
        for c in reversed(range(suf_ref.shape[0])):
            here = suf_ref[c]
            suf_ref[c] = total
            total = total + here
        kv = kv_ref[...].astype(BF16)
        qg = total.astype(BF16)
        for j in range(slots_ref.shape[0]):
            slots_ref[j] = jnp.where(j > me_ref[0], kv, qg)


def sums(me, x, blocks):
    heads = x.shape[0]
    step = CHUNK // ROWS
    chunks = heads // step
    state = (HEAD_DIM, HEAD_DIM)
    whole = lambda i: (0, 0, 0)
    return pl.pallas_call(
        sums_kernel,
        grid=(chunks,),
        in_specs=[
            pl.BlockSpec(memory_space=pltpu.SMEM),
            pl.BlockSpec((step, 4, ROWS, HEAD_DIM), lambda i: (i, 0, 0, 0)),
        ],
        out_specs=[
            pl.BlockSpec((blocks, *state), whole),
            pl.BlockSpec((chunks, *state), whole),
            pl.BlockSpec((chunks, *state), whole),
        ],
        out_shape=[
            jax.ShapeDtypeStruct((blocks, *state), BF16),
            jax.ShapeDtypeStruct((chunks, *state), F32),
            jax.ShapeDtypeStruct((chunks, *state), F32),
        ],
        scratch_shapes=[pltpu.VMEM(state, F32)],
        compiler_params=params("i"),
        name="sums",
    )(me, x)


def near_kernel(me_ref, x_ref, pre_ref, suf_ref, dq_ref, dk_ref, dv_ref):
    q, k, v = part(x_ref, 0), part(x_ref, 1), part(x_ref, 2)
    g = scaled_of(x_ref, me_ref, pl.num_programs(0))
    t = lax.broadcasted_iota(jnp.int32, (CHUNK, CHUNK), 0)
    s = lax.broadcasted_iota(jnp.int32, (CHUNK, CHUNK), 1)
    keep = t >= s
    inner = jnp.where(keep, dot(g, v, 1, 1), 0.0).astype(BF16)
    pairs = jnp.where(keep, dot(q, k, 1, 1), 0.0).astype(BF16)
    pre = split(pre_ref[0])
    suf = split(suf_ref[0])
    dq_ref[...] = dot(inner, k, 1, 0) + (dot(g, pre[0], 1, 1) + dot(g, pre[1], 1, 1))
    dk_ref[...] = dot(inner, q, 0, 0) + (dot(v, suf[0], 1, 1) + dot(v, suf[1], 1, 1))
    dv_ref[...] = dot(pairs, g, 0, 0) + (dot(k, suf[0], 1, 0) + dot(k, suf[1], 1, 0))


def near(me, x, pre, suf):
    heads = x.shape[0]
    step = CHUNK // ROWS
    chunks = heads // step
    state = pl.BlockSpec((1, HEAD_DIM, HEAD_DIM), lambda i: (i, 0, 0))
    rows = pl.BlockSpec((CHUNK, HEAD_DIM), lambda i: (i, 0))
    return pl.pallas_call(
        near_kernel,
        grid=(chunks,),
        in_specs=[
            pl.BlockSpec(memory_space=pltpu.SMEM),
            pl.BlockSpec((step, 4, ROWS, HEAD_DIM), lambda i: (i, 0, 0, 0)),
            state,
            state,
        ],
        out_specs=[rows] * 3,
        out_shape=[jax.ShapeDtypeStruct((chunks * CHUNK, HEAD_DIM), F32)] * 3,
        compiler_params=params("i"),
        cost_estimate=pl.CostEstimate(flops=3_000_000_000, transcendentals=0, bytes_accessed=8 << 20),
        name="near",
    )(me, x, pre, suf)


def far_kernel(me_ref, x_ref, got_ref, dq_ref, dk_ref, dv_ref, o_ref, before_ref, after_ref):
    @pl.when(pl.program_id(0) == 0)
    def _():
        me = me_ref[0]
        before = jnp.zeros((HEAD_DIM, HEAD_DIM), F32)
        after = jnp.zeros((HEAD_DIM, HEAD_DIM), F32)
        for j in range(got_ref.shape[0]):
            here = got_ref[j].astype(F32)
            before = before + jnp.where(j < me, here, 0.0)
            after = after + jnp.where(j > me, here, 0.0)
        for n, value in enumerate(split(before)):
            before_ref[n] = value
        for n, value in enumerate(split(after)):
            after_ref[n] = value

    k, v = part(x_ref, 1), part(x_ref, 2)
    g = scaled_of(x_ref, me_ref, pl.num_programs(0))
    shape = (CHUNK // ROWS, ROWS, HEAD_DIM)
    dq = dq_ref[...] + (dot(g, before_ref[0], 1, 1) + dot(g, before_ref[1], 1, 1))
    dk = dk_ref[...] + (dot(v, after_ref[0], 1, 1) + dot(v, after_ref[1], 1, 1))
    dv = dv_ref[...] + (dot(k, after_ref[0], 1, 0) + dot(k, after_ref[1], 1, 0))
    for a, value in enumerate((dq, dk, dv)):
        o_ref[:, a] = value.astype(BF16).reshape(shape)


def far(me, x, got, dq, dk, dv):
    heads = x.shape[0]
    step = CHUNK // ROWS
    chunks = heads // step
    rows = pl.BlockSpec((CHUNK, HEAD_DIM), lambda i: (i, 0))
    pair = pltpu.VMEM((2, HEAD_DIM, HEAD_DIM), BF16)
    return pl.pallas_call(
        far_kernel,
        grid=(chunks,),
        in_specs=[
            pl.BlockSpec(memory_space=pltpu.SMEM),
            pl.BlockSpec((step, 4, ROWS, HEAD_DIM), lambda i: (i, 0, 0, 0)),
            pl.BlockSpec(got.shape, lambda i: (0, 0, 0)),
            rows,
            rows,
            rows,
        ],
        out_specs=pl.BlockSpec((step, 3, ROWS, HEAD_DIM), lambda i: (i, 0, 0, 0)),
        out_shape=jax.ShapeDtypeStruct((heads, 3, ROWS, HEAD_DIM), BF16),
        scratch_shapes=[pair, pair],
        compiler_params=params("i"),
        name="far",
    )(me, x, got, dq, dk, dv)


def swap(x, axis):
    return lax.all_to_all(x, axis, split_axis=0, concat_axis=0, tiled=True)


def local(queries, key_vectors, value_vectors, out_grad):
    me = lax.axis_index("zh").astype(jnp.int32).reshape(1)
    x = swap(pack(queries, key_vectors, value_vectors, out_grad), GROUP)
    slots, pre, suf = sums(me, x, lax.axis_size("zh"))
    got = swap(slots, "zh")
    dq, dk, dv = near(me, x, pre, suf)
    return tuple(unpack(swap(far(me, x, got, dq, dk, dv), GROUP)))


def solution(mesh):
    fine = Mesh(mesh.devices.reshape(8, 2, 4, 4, 2), AXES)
    spec = P(AXES, None)
    return jax.shard_map(
        local, mesh=fine, in_specs=(spec,) * 4, out_specs=(spec,) * 3, check_vma=False
    )
```

time: 740 us -> 123 us (0.17)
  waiting for transfers between devices: 491 us -> 34.3 us
  other arithmetic: 158 us -> 0 us
  blocking collectives: 0 us -> 32.1 us
  Pallas kernels: 0 us -> 16.9 us
  starting transfers between devices: 39.2 us -> 24.1 us
  between operations: 14.2 us -> 0.72 us
  matrix products: 12 us -> 0 us
    all_gather x2 -> x0, waiting for transfers between devices: 444 us -> none  [carried_in(): everything = lax.all_gather(value, axis)]
    select_n x128 -> x0, other arithmetic: 157 us -> none  [turn(): return jnp.where(reached, new, before)]
    all_to_all x0 -> x1, blocking collectives: none -> 32.1 us  [swap(): return lax.all_to_all(x, axis, split_axis=0, concat_axis=0, tiled=True)]
    pallas_call x0 -> x5, Pallas kernels: none -> 16.9 us  [the longest x1 6.54 us: near(): pl.pallas_call(near_kernel, grid=(chunks,), in_specs=[pl.BlockSpec(memory...]
    all_to_all x7 -> x2, starting transfers between devices: 39.2 us -> 24.1 us  [swap(): return lax.all_to_all(x, axis, split_axis=0, concat_axis=0, tiled=True)]
    all_to_all x7 -> x2, waiting for transfers between devices: 46.4 us -> 34.3 us  [swap(): return lax.all_to_all(x, axis, split_axis=0, concat_axis=0, tiled=True)]
    unnamed x16 -> x28, local copies, waits for them, and re-layouts: 1.5 us -> 13.6 us
    dot_general x9 -> x0, matrix products: 12 us -> none  [the longest x1 3.07 us: local(): jnp.einsum('hts,hsd->htd', inner, kh, preferred_element_type=f32)]
  transfers between devices with their start and end apart: 9 -> 2, of which waited for: 8 -> 2; matrix products, arithmetic and copies ran while one was open for 24% -> 0% of each run, Pallas kernels for 0% -> 5%
where the time goes in v1:
time: 123 us; the launch traced here: 122 us
  waiting for transfers between devices  34.3 us (28%)
  blocking collectives  32.1 us (26%)
  starting transfers between devices  24.1 us (20%)
  Pallas kernels  16.9 us (14%)
  local copies, waits for them, and re-layouts  13.6 us (11%)
    all_to_all x2, waiting for transfers between devices, swap(): return lax.all_to_all(x, axis, split_axis=0, concat_axis=0, tiled=True)  34.3 us
    all_to_all x1, blocking collectives, swap(): return lax.all_to_all(x, axis, split_axis=0, concat_axis=0, tiled=True)  32.1 us
    all_to_all x2, starting transfers between devices, swap(): return lax.all_to_all(x, axis, split_axis=0, concat_axis=0, tiled=True)  24.1 us
    unnamed x28, local copies, waits for them, and re-layouts  13.6 us
    pallas_call x1, Pallas kernels, near(): pl.pallas_call(near_kernel, grid=(chunks,), in_specs=[pl.BlockSpec(memory...  6.54 us
    pallas_call x1, Pallas kernels, far(): pl.pallas_call(far_kernel, grid=(chunks,), in_specs=[pl.BlockSpec(memory_...  5.38 us
    pallas_call x1, Pallas kernels, sums(): pl.pallas_call(sums_kernel, grid=(chunks,), in_specs=[pl.BlockSpec(memory...  2.65 us
  transfers between devices with their start and end apart: 2, of which 2 were waited for; matrix products, arithmetic and copies ran while one was open for 0% of the time, Pallas kernels for 5%

profile of v1, /device:TPU:1, one launch (start us, length us, event | category | flops | bytes accessed | tf_op | source)
XLA Modules:
  0.0 121.8 jit_solution(15375227936522371219)
XLA Ops:
  0.6 0.0 copy-start.6
  0.6 1.0 copy-done.6
  1.7 0.0 copy-start.7
  1.7 1.0 copy-done.7
  2.7 0.0 copy-start.8
  2.7 1.0 copy-done.8
  3.8 0.0 copy-start.9
  3.8 1.0 copy-done.9
  4.8 0.6 pack.1
  5.4 0.0 copy-start.1
  5.4 1.3 %copy-done.1 = bf16[64,4,32,128]{3,2,1,0:T(8,128)(2,1)} copy-done((bf16[64,4,32,128]{3,2,1,0:T(8,128)(2,1)}, bf16[64,4,32,128]{3,2,1,0:T(8,128)(2,1)S(1)}, u32[]{:S(2)}) %copy-start.1) | copy-done | bytes 2097176
  6.8 11.0 %all-to-all-start = ((bf16[64,4,32,128]{3,2,1,0:T(8,128)(2,1)}), bf16[64,4,32,128]{3,2,1,0:T(8,128)(2,1)S(1)}, u32[]{:S(2)}, u32[]{:S(2)}) async-start(bf16[64,4,32,128]{3,2,1,0:T(8,128)(2,1)} %copy-done.1), calls=%async_computation | async-start | bytes 4194304 | tf_op jit(solution)/shard_map/all_to_all | solution.py:230
  17.7 27.9 %all-to-all-done.x_ref = bf16[64,4,32,128]{3,2,1,0:T(8,128)(2,1)S(1)} async-done(((bf16[64,4,32,128]{3,2,1,0:T(8,128)(2,1)}), bf16[64,4,32,128]{3,2,1,0:T(8,128)(2,1)S(1)}, u32[]{:S(2)}, u32[]{:S(2)}) %all-to-all-start) | async-done | bytes 2097184 | tf_op jit(solution)/shard_map/all_to_all | solution.py:230
  45.6 0.0 copy-start
  45.6 2.6 %sums.1 = (bf16[8,128,128]{2,1,0:T(8,128)(2,1)}, f32[8,128,128]{2,1,0:T(8,128)S(1)}, f32[8,128,128]{2,1,0:T(8,128)S(1)}) custom-call(s32[1]{0:T(128)} %bitcast.me_ref, bf16[64,4,32,128]{3,2,1,0:T(8,128)(2,1)S(1)} %all-to-all-done.x_ref), custom_call_target="tpu_custom_call" | custom-call | tf_op jit(solution)/shard_map/sums/pallas_call | solution.py:118
  48.3 0.0 copy-start.10
  48.3 0.8 copy-done.10
  49.1 0.0 copy-start.12
  49.1 0.8 copy-done.12
  49.8 13.2 %all-to-all-start.1 = ((bf16[8,128,128]{2,1,0:T(8,128)(2,1)}), bf16[8,128,128]{2,1,0:T(8,128)(2,1)S(1)}, u32[]{:S(2)}, u32[]{:S(2)}) async-start(bf16[8,128,128]{2,1,0:T(8,128)(2,1)} %get-tuple-element.9), calls=%async_computation.1 | async-start | bytes 524288 | tf_op jit(solution)/shard_map/all_to_all | solution.py:230
  63.0 0.0 copy-done
  63.0 0.0 copy-start.11
  63.0 1.0 copy-done.11
  64.1 0.0 copy-start.13
  64.1 1.0 copy-done.13
  65.1 6.5 %near.1 = (f32[2048,128]{1,0:T(8,128)S(1)}, f32[2048,128]{1,0:T(8,128)S(1)}, f32[2048,128]{1,0:T(8,128)S(1)}) custom-call(s32[1]{0:T(128)} %bitcast.me_ref, bf16[64,4,32,128]{3,2,1,0:T(8,128)(2,1)} %copy-done, f32[8,128,128]{2,1,0:T(8,128)S(1)} %copy-done.11, f32[8,128,128]{2,1,0:T(8,128)S(1)} %copy-done.13), custom_call_target="tpu_custom_call" | custom-call | flops 3000000000 | bytes 8388608 | tf_op jit(solution)/shard_map/near/pallas_call | solution.py:162
  71.7 0.0 copy-start.2
  71.7 1.0 copy-done.2
  72.6 0.0 copy-start.4
  72.6 1.0 copy-done.4
  73.6 6.5 %all-to-all-done.1.got_ref = bf16[8,128,128]{2,1,0:T(8,128)(2,1)S(1)} async-done(((bf16[8,128,128]{2,1,0:T(8,128)(2,1)}), bf16[8,128,128]{2,1,0:T(8,128)(2,1)S(1)}, u32[]{:S(2)}, u32[]{:S(2)}) %all-to-all-start.1) | async-done | bytes 262176 | tf_op jit(solution)/shard_map/all_to_all | solution.py:230
  80.1 0.0 copy-start.3
  80.1 1.2 %copy-done.3 = f32[2048,128]{1,0:T(8,128)S(1)} copy-done((f32[2048,128]{1,0:T(8,128)S(1)}, f32[2048,128]{1,0:T(8,128)}, u32[]{:S(2)}) %copy-start.3) | copy-done | bytes 1048600
  81.3 0.0 copy-start.5
  81.3 1.2 %copy-done.5 = f32[2048,128]{1,0:T(8,128)S(1)} copy-done((f32[2048,128]{1,0:T(8,128)S(1)}, f32[2048,128]{1,0:T(8,128)}, u32[]{:S(2)}) %copy-start.5) | copy-done | bytes 1048600
  82.5 5.4 %far.1 = bf16[64,3,32,128]{3,2,1,0:T(8,128)(2,1)S(1)} custom-call(s32[1]{0:T(128)} %bitcast.me_ref, bf16[64,4,32,128]{3,2,1,0:T(8,128)(2,1)} %copy-done, bf16[8,128,128]{2,1,0:T(8,128)(2,1)S(1)} %all-to-all-done.1.got_ref, f32[2048,128]{1,0:T(8,128)S(1)} %get-tuple-element.12.dq_ref, f32[2048,128]{1,0:T(8,128)S(1)} %copy-done.3, f32[2048,128]{1,0:T(8,128)S(1)} %copy-done.5), custom_call_target="tpu_custom_call" | custom-call | tf_op jit(solution)/shard_map/far/pallas_call | solution.py:210
  87.9 32.1 %all_to_all.15.x_ref = bf16[64,3,32,128]{3,2,1,0:T(8,128)(2,1)S(1)} all-to-all(bf16[64,3,32,128]{3,2,1,0:T(8,128)(2,1)S(1)} %far.1), channel_id=1, replica_groups=mesh['zh'=8,'zl'=2,'x'=4,'y'=4,'c'=2] {'zl','x','y','c'}, dimensions={0} | all-to-all | bytes 3145728 | tf_op jit(solution)/shard_map/all_to_all | solution.py:230
  120.0 1.7 %unpack.1 = (bf16[32,8192]{1,0:T(8,128)(2,1)}, bf16[32,8192]{1,0:T(8,128)(2,1)}, bf16[32,8192]{1,0:T(8,128)(2,1)}) custom-call(bf16[64,3,32,128]{3,2,1,0:T(8,128)(2,1)S(1)} %all_to_all.15.x_ref), custom_call_target="tpu_custom_call" | custom-call | tf_op jit(solution)/shard_map/unpack/pallas_call | solution.py:64
Async XLA Ops:
  0.6 1.0 copy-start.6
  1.7 1.0 copy-start.7
  2.7 1.0 copy-start.8
  3.8 1.0 copy-start.9
  5.4 1.3 %copy-start.1 = (bf16[64,4,32,128]{3,2,1,0:T(8,128)(2,1)}, bf16[64,4,32,128]{3,2,1,0:T(8,128)(2,1)S(1)}, u32[]{:S(2)}) copy-start(bf16[64,4,32,128]{3,2,1,0:T(8,128)(2,1)S(1)} %pack.1) | copy-start | bytes 6291460
  6.8 38.9 %all-to-all-start = ((bf16[64,4,32,128]{3,2,1,0:T(8,128)(2,1)}), bf16[64,4,32,128]{3,2,1,0:T(8,128)(2,1)S(1)}, u32[]{:S(2)}, u32[]{:S(2)}) async-start(bf16[64,4,32,128]{3,2,1,0:T(8,128)(2,1)} %copy-done.1), calls=%async_computation | async-start | bytes 4194304 | tf_op jit(solution)/shard_map/all_to_all | solution.py:230
  45.6 17.4 %copy-start = (bf16[64,4,32,128]{3,2,1,0:T(8,128)(2,1)}, bf16[64,4,32,128]{3,2,1,0:T(8,128)(2,1)S(1)}, u32[]{:S(2)}) copy-start(bf16[64,4,32,128]{3,2,1,0:T(8,128)(2,1)S(1)} %all-to-all-done.x_ref) | copy-start | bytes 6291460
  48.3 0.8 copy-start.10
  49.1 0.8 copy-start.12
  49.8 30.2 %all-to-all-start.1 = ((bf16[8,128,128]{2,1,0:T(8,128)(2,1)}), bf16[8,128,128]{2,1,0:T(8,128)(2,1)S(1)}, u32[]{:S(2)}, u32[]{:S(2)}) async-start(bf16[8,128,128]{2,1,0:T(8,128)(2,1)} %get-tuple-element.9), calls=%async_computation.1 | async-start | bytes 524288 | tf_op jit(solution)/shard_map/all_to_all | solution.py:230
  63.0 1.0 copy-start.11
  64.1 1.0 copy-start.13
  71.7 1.0 copy-start.2
  72.6 1.0 copy-start.4
  80.1 1.2 %copy-start.3 = (f32[2048,128]{1,0:T(8,128)S(1)}, f32[2048,128]{1,0:T(8,128)}, u32[]{:S(2)}) copy-start(f32[2048,128]{1,0:T(8,128)} %copy-done.2) | copy-start | bytes 3145732
  81.3 1.2 %copy-start.5 = (f32[2048,128]{1,0:T(8,128)S(1)}, f32[2048,128]{1,0:T(8,128)}, u32[]{:S(2)}) copy-start(f32[2048,128]{1,0:T(8,128)} %copy-done.4) | copy-start | bytes 3145732

commit v2 on v1

v2 whole, which is shorter than its diff:
```python
import jax
import jax.numpy as jnp
from jax import lax
from jax.experimental import pallas as pl
from jax.experimental.pallas import tpu as pltpu
from jax.sharding import Mesh, PartitionSpec as P

HEAD_DIM = 128
ROWS = 32
CHUNK = 256
STEP = CHUNK // ROWS
PIECES = 4
AXES = ("zh", "zl", "x", "y", "c")
GROUP = ("zl", "x", "y", "c")
F32 = jnp.float32
BF16 = jnp.bfloat16


def dot(a, b, ca, cb):
    return lax.dot_general(a, b, (((ca,), (cb,)), ((), ())), preferred_element_type=F32)


def params(*names):
    return pltpu.CompilerParams(
        dimension_semantics=("arbitrary",) * len(names), vmem_limit_bytes=16 * 1024 * 1024
    )


def split(x):
    high = x.astype(BF16)
    return high, (x - high.astype(F32)).astype(BF16)


def pack_kernel(first_ref, *refs):
    ins, (o_ref, held, made, in_sem, out_sem) = refs[:4], refs[4:]
    _, rows, width = held.shape
    columns = width // PIECES
    heads = columns // HEAD_DIM

    def fetch(p, a):
        at = (slice(None), pl.ds(p * columns, columns))
        return pltpu.make_async_copy(ins[a].at[at], held.at[(a, *at)], in_sem.at[p, a])

    def send(p):
        at = pl.ds(p * heads, heads)
        return pltpu.make_async_copy(made.at[at], o_ref.at[at], out_sem.at[p])

    for p in range(PIECES):
        for a in range(4):
            fetch(p, a).start()
    place = lax.broadcasted_iota(jnp.int32, (rows, HEAD_DIM), 0) + first_ref[0]
    factor = lax.rsqrt(HEAD_DIM * (place.astype(F32) + 1.0))
    for p in range(PIECES):
        for a in range(4):
            fetch(p, a).wait()
        for h in range(p * heads, (p + 1) * heads):
            at = slice(h * HEAD_DIM, (h + 1) * HEAD_DIM)
            made[h, 0] = held[0, :, at]
            made[h, 1] = held[1, :, at]
            made[h, 2] = (held[2, :, at].astype(F32) * factor).astype(BF16)
            made[h, 3] = held[3, :, at]
        send(p).start()
    for p in range(PIECES):
        send(p).wait()


def pack(first, *arrays):
    rows, width = arrays[0].shape
    shape = (width // HEAD_DIM, 4, rows, HEAD_DIM)
    arrays = [pltpu.with_memory_space_constraint(y, pltpu.HBM) for y in arrays]
    return pl.pallas_call(
        pack_kernel,
        in_specs=[pl.BlockSpec(memory_space=pltpu.SMEM)]
        + [pl.BlockSpec(memory_space=pltpu.HBM)] * 4,
        out_specs=pl.BlockSpec(memory_space=pltpu.HBM),
        out_shape=pltpu.HBM(shape, BF16),
        scratch_shapes=[
            pltpu.VMEM((4, rows, width), BF16),
            pltpu.VMEM(shape, BF16),
            pltpu.SemaphoreType.DMA((PIECES, 4)),
            pltpu.SemaphoreType.DMA((PIECES,)),
        ],
        compiler_params=params(),
        name="pack",
    )(first, *arrays)


def unpack_kernel(x_ref, *refs):
    outs, (made, sem) = refs[:3], refs[3:]
    width = made.shape[2]
    columns = width // PIECES
    heads = columns // HEAD_DIM

    def send(p, a):
        at = (slice(None), pl.ds(p * columns, columns))
        return pltpu.make_async_copy(made.at[(a, *at)], outs[a].at[at], sem.at[p, a])

    for p in range(PIECES):
        for a in range(3):
            for h in range(p * heads, (p + 1) * heads):
                made[a, :, h * HEAD_DIM : (h + 1) * HEAD_DIM] = x_ref[h, a]
            send(p, a).start()
    for p in range(PIECES):
        for a in range(3):
            send(p, a).wait()


def unpack(x):
    heads, n, rows, _ = x.shape
    width = heads * HEAD_DIM
    return pl.pallas_call(
        unpack_kernel,
        in_specs=[pl.BlockSpec(memory_space=pltpu.VMEM)],
        out_specs=[pl.BlockSpec(memory_space=pltpu.HBM)] * n,
        out_shape=[pltpu.HBM((rows, width), x.dtype)] * n,
        scratch_shapes=[
            pltpu.VMEM((n, rows, width), x.dtype),
            pltpu.SemaphoreType.DMA((PIECES, n)),
        ],
        compiler_params=params(),
        name="unpack",
    )(x)


def rows_of(x_ref, a, c=None):
    x = x_ref[:, a] if c is None else x_ref[c * STEP : (c + 1) * STEP, a]
    return x.reshape(-1, HEAD_DIM)


def sums_kernel(me_ref, x_ref, slots_ref):
    kv = dot(rows_of(x_ref, 0), rows_of(x_ref, 1), 0, 0).astype(BF16)
    qg = dot(rows_of(x_ref, 3), rows_of(x_ref, 2), 0, 0).astype(BF16)
    for j in range(slots_ref.shape[0]):
        slots_ref[j] = jnp.where(j > me_ref[0], kv, qg)


def sums(me, x, blocks):
    return pl.pallas_call(
        sums_kernel,
        in_specs=[
            pl.BlockSpec(memory_space=pltpu.SMEM),
            pl.BlockSpec(memory_space=pltpu.VMEM),
        ],
        out_specs=pl.BlockSpec(memory_space=pltpu.VMEM),
        out_shape=jax.ShapeDtypeStruct((blocks, HEAD_DIM, HEAD_DIM), BF16),
        compiler_params=params(),
        name="sums",
    )(me, x)


def near_kernel(x_ref, dq_ref, dk_ref, dv_ref, kv_ref, suf_ref):
    i = pl.program_id(0)
    chunks = suf_ref.shape[0]

    @pl.when(i == 0)
    def _():
        kv_ref[...] = jnp.zeros_like(kv_ref)
        after = jnp.zeros((HEAD_DIM, HEAD_DIM), F32)
        for c in reversed(range(chunks)):
            suf_ref[c] = after
            if c:
                after = after + dot(rows_of(x_ref, 3, c), rows_of(x_ref, 2, c), 0, 0)

    at = pl.ds(i * STEP, STEP)
    k, v, g, q = (x_ref[at, a].reshape(CHUNK, HEAD_DIM) for a in range(4))
    t = lax.broadcasted_iota(jnp.int32, (CHUNK, CHUNK), 0)
    s = lax.broadcasted_iota(jnp.int32, (CHUNK, CHUNK), 1)
    keep = t >= s
    inner = jnp.where(keep, dot(g, v, 1, 1), 0.0).astype(BF16)
    pairs = jnp.where(keep, dot(q, k, 1, 1), 0.0).astype(BF16)
    pre = split(kv_ref[...])
    suf = split(suf_ref[i])
    dq_ref[...] = dot(inner, k, 1, 0) + (dot(g, pre[0], 1, 1) + dot(g, pre[1], 1, 1))
    dk_ref[...] = dot(inner, q, 0, 0) + (dot(v, suf[0], 1, 1) + dot(v, suf[1], 1, 1))
    dv_ref[...] = dot(pairs, g, 0, 0) + (dot(k, suf[0], 1, 0) + dot(k, suf[1], 1, 0))
    kv_ref[...] += dot(k, v, 0, 0)


def near(x):
    chunks = x.shape[0] // STEP
    rows = pl.BlockSpec((CHUNK, HEAD_DIM), lambda i: (i, 0))
    return pl.pallas_call(
        near_kernel,
        grid=(chunks,),
        in_specs=[pl.BlockSpec(memory_space=pltpu.VMEM)],
        out_specs=[rows] * 3,
        out_shape=[pltpu.HBM((chunks * CHUNK, HEAD_DIM), F32)] * 3,
        scratch_shapes=[
            pltpu.VMEM((HEAD_DIM, HEAD_DIM), F32),
            pltpu.VMEM((chunks, HEAD_DIM, HEAD_DIM), F32),
        ],
        compiler_params=params("i"),
        cost_estimate=pl.CostEstimate(flops=3_000_000_000, transcendentals=0, bytes_accessed=8 << 20),
        name="near",
    )(x)


def far_kernel(me_ref, x_ref, got_ref, *refs):
    ins, (o_ref, held, dq_state, dk_state, dv_state, sem) = refs[:3], refs[3:]
    heads = o_ref.shape[0] // PIECES
    rows = heads * ROWS

    def fetch(p, a):
        at = pl.ds(p * rows, rows)
        return pltpu.make_async_copy(ins[a].at[at], held.at[a, at], sem.at[p, a])

    for p in range(PIECES):
        for a in range(3):
            fetch(p, a).start()
    me = me_ref[0]
    before = jnp.zeros((HEAD_DIM, HEAD_DIM), F32)
    after = jnp.zeros((HEAD_DIM, HEAD_DIM), F32)
    for j in range(got_ref.shape[0]):
        here = got_ref[j].astype(F32)
        before = before + jnp.where(j < me, here, 0.0)
        after = after + jnp.where(j > me, here, 0.0)
    for n, (b, s) in enumerate(zip(split(before), split(after))):
        at = slice(n * HEAD_DIM, (n + 1) * HEAD_DIM)
        dq_state[:, at] = b
        dk_state[:, at] = s
        dv_state[at, :] = s
    for p in range(PIECES):
        for a in range(3):
            fetch(p, a).wait()
        hs = slice(p * heads, (p + 1) * heads)
        rs = slice(p * rows, (p + 1) * rows)
        k, v, g = (x_ref[hs, a].reshape(rows, HEAD_DIM) for a in range(3))
        k, v, g = (jnp.concatenate([y, y], axis=1) for y in (k, v, g))
        dq = held[0, rs] + dot(g, dq_state[...], 1, 1)
        dk = held[1, rs] + dot(v, dk_state[...], 1, 1)
        dv = held[2, rs] + dot(k, dv_state[...], 1, 0)
        for a, value in enumerate((dq, dk, dv)):
            o_ref[hs, a] = value.astype(BF16).reshape(heads, ROWS, HEAD_DIM)


def far(me, x, got, *parts):
    heads = x.shape[0]
    vmem = pl.BlockSpec(memory_space=pltpu.VMEM)
    parts = [pltpu.with_memory_space_constraint(y, pltpu.HBM) for y in parts]
    wide = pltpu.VMEM((HEAD_DIM, 2 * HEAD_DIM), BF16)
    return pl.pallas_call(
        far_kernel,
        in_specs=[pl.BlockSpec(memory_space=pltpu.SMEM), vmem, vmem]
        + [pl.BlockSpec(memory_space=pltpu.HBM)] * 3,
        out_specs=vmem,
        out_shape=jax.ShapeDtypeStruct((heads, 3, ROWS, HEAD_DIM), BF16),
        scratch_shapes=[
            pltpu.VMEM((3, heads * ROWS, HEAD_DIM), F32),
            wide,
            wide,
            pltpu.VMEM((2 * HEAD_DIM, HEAD_DIM), BF16),
            pltpu.SemaphoreType.DMA((PIECES, 3)),
        ],
        compiler_params=params(),
        name="far",
    )(me, x, got, *parts)


def swap(x, axis):
    return lax.all_to_all(x, axis, split_axis=0, concat_axis=0, tiled=True)


def local(queries, key_vectors, value_vectors, out_grad):
    me = lax.axis_index("zh").astype(jnp.int32).reshape(1)
    first = (lax.axis_index(AXES) * ROWS).astype(jnp.int32).reshape(1)
    x = swap(pack(first, key_vectors, value_vectors, out_grad, queries), GROUP)
    got = swap(sums(me, x, lax.axis_size("zh")), "zh")
    dq, dk, dv = near(x)
    return tuple(unpack(swap(far(me, x, got, dq, dk, dv), GROUP)))


def solution(mesh):
    fine = Mesh(mesh.devices.reshape(8, 2, 4, 4, 2), AXES)
    spec = P(AXES, None)
    return jax.shard_map(
        local, mesh=fine, in_specs=(spec,) * 4, out_specs=(spec,) * 3, check_vma=False
    )
```

time: 123 us -> 110 us (0.89)
  blocking collectives: 32.1 us -> 71.1 us
  waiting for transfers between devices: 34.3 us -> 11.4 us
  local copies, waits for them, and re-layouts: 13.6 us -> 0 us
  starting transfers between devices: 24.1 us -> 13.1 us
  Pallas kernels: 16.9 us -> 13.8 us
    all_to_all x1 -> x2, blocking collectives: 32.1 us -> 71.1 us  [swap(): return lax.all_to_all(x, axis, split_axis=0, concat_axis=0, tiled=True)]
    all_to_all x2 -> x1, waiting for transfers between devices: 34.3 us -> 11.4 us  [swap(): return lax.all_to_all(x, axis, split_axis=0, concat_axis=0, tiled=True)]
    unnamed x28 -> x0, local copies, waits for them, and re-layouts: 13.6 us -> none
    all_to_all x2 -> x1, starting transfers between devices: 24.1 us -> 13.1 us  [swap(): return lax.all_to_all(x, axis, split_axis=0, concat_axis=0, tiled=True)]
    pallas_call x4, Pallas kernels: 10.4 us -> 8.13 us  [the longest x1 2.97 us: far(): pl.pallas_call(far_kernel, in_specs=[pl.BlockSpec(memory_space=pltpu.SMEM...]
  transfers between devices with their start and end apart: 2 -> 1, of which waited for: 2 -> 1; matrix products, arithmetic and copies ran while one was open for 0% -> 0% of each run, Pallas kernels for 5% -> 5%
where the time goes in v2:
time: 110 us
  blocking collectives  71.1 us (65%)
  Pallas kernels  13.8 us (13%)
  starting transfers between devices  13.1 us (12%)
  waiting for transfers between devices  11.4 us (10%)
    all_to_all x2, blocking collectives, swap(): return lax.all_to_all(x, axis, split_axis=0, concat_axis=0, tiled=True)  71.1 us
    all_to_all x1, starting transfers between devices, swap(): return lax.all_to_all(x, axis, split_axis=0, concat_axis=0, tiled=True)  13.1 us
    all_to_all x1, waiting for transfers between devices, swap(): return lax.all_to_all(x, axis, split_axis=0, concat_axis=0, tiled=True)  11.4 us
    pallas_call x1, Pallas kernels, near(): pl.pallas_call(near_kernel, grid=(chunks,), in_specs=[pl.BlockSpec(memory...  5.64 us
    pallas_call x1, Pallas kernels, far(): pl.pallas_call(far_kernel, in_specs=[pl.BlockSpec(memory_space=pltpu.SMEM...  2.97 us
    pallas_call x1, Pallas kernels, pack(): pl.pallas_call(pack_kernel, in_specs=[pl.BlockSpec(memory_space=pltpu.SME...  2.72 us
  transfers between devices with their start and end apart: 1, of which 1 were waited for; matrix products, arithmetic and copies ran while one was open for 0% of the time, Pallas kernels for 5%

profile of v2, /device:TPU:1, one launch (start us, length us, event | category | flops | bytes accessed | tf_op | source)
XLA Modules:
  0.0 110.0 jit_solution(11428666302430652636)
XLA Ops:
  0.6 2.7 %pack.1 = bf16[64,4,32,128]{3,2,1,0:T(8,128)(2,1)} custom-call(s32[1]{0:T(128)} %bitcast.1.first_ref, bf16[32,8192]{1,0:T(8,128)(2,1)} %refs_0_.1, bf16[32,8192]{1,0:T(8,128)(2,1)} %refs_1_.1, bf16[32,8192]{1,0:T(8,128)(2,1)} %refs_2_.1, bf16[32,8192]{1,0:T(8,128)(2,1)} %refs_3_.1), custom_call_target="tpu_custom_call" | custom-call | tf_op jit(solution)/shard_map/pack/pallas_call | solution.py:71
  3.4 38.9 %all_to_all.15.x_ref = bf16[64,4,32,128]{3,2,1,0:T(8,128)(2,1)S(1)} all-to-all(bf16[64,4,32,128]{3,2,1,0:T(8,128)(2,1)} %pack.1), channel_id=1, replica_groups=mesh['zh'=8,'zl'=2,'x'=4,'y'=4,'c'=2] {'zl','x','y','c'}, dimensions={0} | all-to-all | bytes 4194304 | tf_op jit(solution)/shard_map/all_to_all | solution.py:260
  42.3 1.2 %sums.1 = bf16[8,128,128]{2,1,0:T(8,128)(2,1)} custom-call(s32[1]{0:T(128)} %bitcast.me_ref, bf16[64,4,32,128]{3,2,1,0:T(8,128)(2,1)S(1)} %all_to_all.15.x_ref), custom_call_target="tpu_custom_call" | custom-call | tf_op jit(solution)/shard_map/sums/pallas_call | solution.py:138
  43.5 13.1 %all-to-all-start.1 = ((bf16[8,128,128]{2,1,0:T(8,128)(2,1)}), bf16[8,128,128]{2,1,0:T(8,128)(2,1)S(1)}, u32[]{:S(2)}, u32[]{:S(2)}) async-start(bf16[8,128,128]{2,1,0:T(8,128)(2,1)} %sums.1), calls=%async_computation.1 | async-start | bytes 524288 | tf_op jit(solution)/shard_map/all_to_all | solution.py:260
  56.6 5.6 %near.1 = (f32[2048,128]{1,0:T(8,128)}, f32[2048,128]{1,0:T(8,128)}, f32[2048,128]{1,0:T(8,128)}) custom-call(bf16[64,4,32,128]{3,2,1,0:T(8,128)(2,1)S(1)} %all_to_all.15.x_ref), custom_call_target="tpu_custom_call" | custom-call | flops 3000000000 | bytes 8388608 | tf_op jit(solution)/shard_map/near/pallas_call | solution.py:182
  62.2 11.4 %all-to-all-done.1.got_ref = bf16[8,128,128]{2,1,0:T(8,128)(2,1)S(1)} async-done(((bf16[8,128,128]{2,1,0:T(8,128)(2,1)}), bf16[8,128,128]{2,1,0:T(8,128)(2,1)S(1)}, u32[]{:S(2)}, u32[]{:S(2)}) %all-to-all-start.1) | async-done | bytes 262176 | tf_op jit(solution)/shard_map/all_to_all | solution.py:260
  73.6 3.0 %far.1 = bf16[64,3,32,128]{3,2,1,0:T(8,128)(2,1)S(1)} custom-call(s32[1]{0:T(128)} %bitcast.me_ref, bf16[64,4,32,128]{3,2,1,0:T(8,128)(2,1)S(1)} %all_to_all.15.x_ref, bf16[8,128,128]{2,1,0:T(8,128)(2,1)S(1)} %all-to-all-done.1.got_ref, f32[2048,128]{1,0:T(8,128)} %get-tuple-element.6.refs_0_, f32[2048,128]{1,0:T(8,128)} %get-tuple-element.7.refs_1_, ...), custom_call_target="tpu_custom_call" | custom-call | tf_op jit(solution)/shard_map/far/pallas_call | solution.py:241
  76.6 32.1 %all_to_all.16.x_ref = bf16[64,3,32,128]{3,2,1,0:T(8,128)(2,1)S(1)} all-to-all(bf16[64,3,32,128]{3,2,1,0:T(8,128)(2,1)S(1)} %far.1), channel_id=1, replica_groups=mesh['zh'=8,'zl'=2,'x'=4,'y'=4,'c'=2] {'zl','x','y','c'}, dimensions={0} | all-to-all | bytes 3145728 | tf_op jit(solution)/shard_map/all_to_all | solution.py:260
  108.8 1.3 %unpack.1 = (bf16[32,8192]{1,0:T(8,128)(2,1)}, bf16[32,8192]{1,0:T(8,128)(2,1)}, bf16[32,8192]{1,0:T(8,128)(2,1)}) custom-call(bf16[64,3,32,128]{3,2,1,0:T(8,128)(2,1)S(1)} %all_to_all.16.x_ref), custom_call_target="tpu_custom_call" | custom-call | tf_op jit(solution)/shard_map/unpack/pallas_call | solution.py:111
Async XLA Ops:
  43.5 30.2 %all-to-all-start.1 = ((bf16[8,128,128]{2,1,0:T(8,128)(2,1)}), bf16[8,128,128]{2,1,0:T(8,128)(2,1)S(1)}, u32[]{:S(2)}, u32[]{:S(2)}) async-start(bf16[8,128,128]{2,1,0:T(8,128)(2,1)} %sums.1), calls=%async_computation.1 | async-start | bytes 524288 | tf_op jit(solution)/shard_map/all_to_all | solution.py:260

commit v3 on v2

--- a/solution.py
+++ b/solution.py
@@ -10,8 +10,9 @@
 CHUNK = 256
 STEP = CHUNK // ROWS
 PIECES = 4
-AXES = ("zh", "zl", "x", "y", "c")
-GROUP = ("zl", "x", "y", "c")
+BLOCKS = "block"
+GROUP = "group"
+AXES = (BLOCKS, GROUP)
 F32 = jnp.float32
 BF16 = jnp.bfloat16
 
@@ -184,7 +185,8 @@
         grid=(chunks,),
         in_specs=[pl.BlockSpec(memory_space=pltpu.VMEM)],
         out_specs=[rows] * 3,
-        out_shape=[pltpu.HBM((chunks * CHUNK, HEAD_DIM), F32)] * 3,
+        out_shape=[jax.ShapeDtypeStruct((chunks * CHUNK, HEAD_DIM), F32)]
+        + [pltpu.HBM((chunks * CHUNK, HEAD_DIM), F32)] * 2,
         scratch_shapes=[
             pltpu.VMEM((HEAD_DIM, HEAD_DIM), F32),
             pltpu.VMEM((chunks, HEAD_DIM, HEAD_DIM), F32),
@@ -195,18 +197,14 @@
     )(x)
 
 
-def far_kernel(me_ref, x_ref, got_ref, *refs):
-    ins, (o_ref, held, dq_state, dk_state, dv_state, sem) = refs[:3], refs[3:]
-    heads = o_ref.shape[0] // PIECES
-    rows = heads * ROWS
-
-    def fetch(p, a):
-        at = pl.ds(p * rows, rows)
-        return pltpu.make_async_copy(ins[a].at[at], held.at[a, at], sem.at[p, a])
-
-    for p in range(PIECES):
-        for a in range(3):
-            fetch(p, a).start()
+def far_kernel(me_ref, x_ref, got_ref, dq_ref, *refs):
+    ins, (o_ref, held, dq_state, dk_state, dv_state, sem) = refs[:2], refs[2:]
+
+    def fetch(a):
+        return pltpu.make_async_copy(ins[a], held.at[a], sem.at[a])
+
+    for a in range(2):
+        fetch(a).start()
     me = me_ref[0]
     before = jnp.zeros((HEAD_DIM, HEAD_DIM), F32)
     after = jnp.zeros((HEAD_DIM, HEAD_DIM), F32)
@@ -219,41 +217,41 @@
         dq_state[:, at] = b
         dk_state[:, at] = s
         dv_state[at, :] = s
-    for p in range(PIECES):
-        for a in range(3):
-            fetch(p, a).wait()
-        hs = slice(p * heads, (p + 1) * heads)
-        rs = slice(p * rows, (p + 1) * rows)
-        k, v, g = (x_ref[hs, a].reshape(rows, HEAD_DIM) for a in range(3))
-        k, v, g = (jnp.concatenate([y, y], axis=1) for y in (k, v, g))
-        dq = held[0, rs] + dot(g, dq_state[...], 1, 1)
-        dk = held[1, rs] + dot(v, dk_state[...], 1, 1)
-        dv = held[2, rs] + dot(k, dv_state[...], 1, 0)
-        for a, value in enumerate((dq, dk, dv)):
-            o_ref[hs, a] = value.astype(BF16).reshape(heads, ROWS, HEAD_DIM)
-
-
-def far(me, x, got, *parts):
+
+    def add(out, source, near, state, axis):
+        y = rows_of(x_ref, source)
+        y = jnp.concatenate([y, y], axis=1)
+        value = near[...] + dot(y, state[...], 1, axis)
+        o_ref[:, out] = value.astype(BF16).reshape(-1, ROWS, HEAD_DIM)
+
+    add(0, 2, dq_ref, dq_state, 1)
+    for a in range(2):
+        fetch(a).wait()
+    add(1, 1, held.at[0], dk_state, 1)
+    add(2, 0, held.at[1], dv_state, 0)
+
+
+def far(me, x, got, dq, *parts):
     heads = x.shape[0]
     vmem = pl.BlockSpec(memory_space=pltpu.VMEM)
     parts = [pltpu.with_memory_space_constraint(y, pltpu.HBM) for y in parts]
     wide = pltpu.VMEM((HEAD_DIM, 2 * HEAD_DIM), BF16)
     return pl.pallas_call(
         far_kernel,
-        in_specs=[pl.BlockSpec(memory_space=pltpu.SMEM), vmem, vmem]
-        + [pl.BlockSpec(memory_space=pltpu.HBM)] * 3,
+        in_specs=[pl.BlockSpec(memory_space=pltpu.SMEM), vmem, vmem, vmem]
+        + [pl.BlockSpec(memory_space=pltpu.HBM)] * 2,
         out_specs=vmem,
         out_shape=jax.ShapeDtypeStruct((heads, 3, ROWS, HEAD_DIM), BF16),
         scratch_shapes=[
-            pltpu.VMEM((3, heads * ROWS, HEAD_DIM), F32),
+            pltpu.VMEM((2, heads * ROWS, HEAD_DIM), F32),
             wide,
             wide,
             pltpu.VMEM((2 * HEAD_DIM, HEAD_DIM), BF16),
-            pltpu.SemaphoreType.DMA((PIECES, 3)),
+            pltpu.SemaphoreType.DMA((2,)),
         ],
         compiler_params=params(),
         name="far",
-    )(me, x, got, *parts)
+    )(me, x, got, dq, *parts)
 
 
 def swap(x, axis):
@@ -261,16 +259,15 @@
 
 
 def local(queries, key_vectors, value_vectors, out_grad):
-    me = lax.axis_index("zh").astype(jnp.int32).reshape(1)
+    me = lax.axis_index(BLOCKS).astype(jnp.int32).reshape(1)
     first = (lax.axis_index(AXES) * ROWS).astype(jnp.int32).reshape(1)
     x = swap(pack(first, key_vectors, value_vectors, out_grad, queries), GROUP)
-    got = swap(sums(me, x, lax.axis_size("zh")), "zh")
-    dq, dk, dv = near(x)
-    return tuple(unpack(swap(far(me, x, got, dq, dk, dv), GROUP)))
+    got = swap(sums(me, x, lax.axis_size(BLOCKS)), BLOCKS)
+    return tuple(unpack(swap(far(me, x, got, *near(x)), GROUP)))
 
 
 def solution(mesh):
-    fine = Mesh(mesh.devices.reshape(8, 2, 4, 4, 2), AXES)
+    fine = Mesh(mesh.devices.reshape(8, 64), AXES)
     spec = P(AXES, None)
     return jax.shard_map(
         local, mesh=fine, in_specs=(spec,) * 4, out_specs=(spec,) * 3, check_vma=False

time: 110 us -> 110 us (level)
  no operation moved by 1% of the time
where the time goes in v3:
time: 110 us; the launch traced here: 109 us
  blocking collectives  71 us (65%)
  Pallas kernels  13.1 us (12%)
  starting transfers between devices  13.1 us (12%)
  waiting for transfers between devices  11.4 us (10%)
    all_to_all x2, blocking collectives, swap(): return lax.all_to_all(x, axis, split_axis=0, concat_axis=0, tiled=True)  71 us
    all_to_all x1, starting transfers between devices, swap(): return lax.all_to_all(x, axis, split_axis=0, concat_axis=0, tiled=True)  13.1 us
    all_to_all x1, waiting for transfers between devices, swap(): return lax.all_to_all(x, axis, split_axis=0, concat_axis=0, tiled=True)  11.4 us
    pallas_call x1, Pallas kernels, near(): pl.pallas_call(near_kernel, grid=(chunks,), in_specs=[pl.BlockSpec(memory...  5.62 us
    pallas_call x1, Pallas kernels, pack(): pl.pallas_call(pack_kernel, in_specs=[pl.BlockSpec(memory_space=pltpu.SME...  2.72 us
    pallas_call x1, Pallas kernels, far(): pl.pallas_call(far_kernel, in_specs=[pl.BlockSpec(memory_space=pltpu.SMEM...  2.28 us
  transfers between devices with their start and end apart: 1, of which 1 were waited for; matrix products, arithmetic and copies ran while one was open for 0% of the time, Pallas kernels for 5%

profile of v3, /device:TPU:1, one launch (start us, length us, event | category | flops | bytes accessed | tf_op | source)
XLA Modules:
  0.0 109.3 jit_solution(12265135533336760858)
XLA Ops:
  0.6 2.7 %pack.1 = bf16[64,4,32,128]{3,2,1,0:T(8,128)(2,1)} custom-call(s32[1]{0:T(128)} %bitcast.1.first_ref, bf16[32,8192]{1,0:T(8,128)(2,1)} %refs_0_.1, bf16[32,8192]{1,0:T(8,128)(2,1)} %refs_1_.1, bf16[32,8192]{1,0:T(8,128)(2,1)} %refs_2_.1, bf16[32,8192]{1,0:T(8,128)(2,1)} %refs_3_.1), custom_call_target="tpu_custom_call" | custom-call | tf_op jit(solution)/shard_map/pack/pallas_call | solution.py:72
  3.4 38.9 %all_to_all.15.x_ref = bf16[64,4,32,128]{3,2,1,0:T(8,128)(2,1)S(1)} all-to-all(bf16[64,4,32,128]{3,2,1,0:T(8,128)(2,1)} %pack.1), channel_id=1, replica_groups=mesh['seq'=64,'head'=8] {'seq':(8)8,'head'}, dimensions={0} | all-to-all | bytes 4194304 | tf_op jit(solution)/shard_map/all_to_all | solution.py:258
  42.3 1.2 %sums.1 = bf16[8,128,128]{2,1,0:T(8,128)(2,1)} custom-call(s32[1]{0:T(128)} %bitcast.me_ref, bf16[64,4,32,128]{3,2,1,0:T(8,128)(2,1)S(1)} %all_to_all.15.x_ref), custom_call_target="tpu_custom_call" | custom-call | tf_op jit(solution)/shard_map/sums/pallas_call | solution.py:139
  43.5 13.1 %all-to-all-start.1 = ((bf16[8,128,128]{2,1,0:T(8,128)(2,1)}), bf16[8,128,128]{2,1,0:T(8,128)(2,1)S(1)}, u32[]{:S(2)}, u32[]{:S(2)}) async-start(bf16[8,128,128]{2,1,0:T(8,128)(2,1)} %sums.1), calls=%async_computation.1 | async-start | bytes 524288 | tf_op jit(solution)/shard_map/all_to_all | solution.py:258
  56.6 5.6 %near.1 = (f32[2048,128]{1,0:T(8,128)S(1)}, f32[2048,128]{1,0:T(8,128)}, f32[2048,128]{1,0:T(8,128)}) custom-call(bf16[64,4,32,128]{3,2,1,0:T(8,128)(2,1)S(1)} %all_to_all.15.x_ref), custom_call_target="tpu_custom_call" | custom-call | flops 3000000000 | bytes 8388608 | tf_op jit(solution)/shard_map/near/pallas_call | solution.py:183
  62.2 11.4 %all-to-all-done.1.got_ref = bf16[8,128,128]{2,1,0:T(8,128)(2,1)S(1)} async-done(((bf16[8,128,128]{2,1,0:T(8,128)(2,1)}), bf16[8,128,128]{2,1,0:T(8,128)(2,1)S(1)}, u32[]{:S(2)}, u32[]{:S(2)}) %all-to-all-start.1) | async-done | bytes 262176 | tf_op jit(solution)/shard_map/all_to_all | solution.py:258
  73.6 2.3 %far.1 = bf16[64,3,32,128]{3,2,1,0:T(8,128)(2,1)S(1)} custom-call(s32[1]{0:T(128)} %bitcast.me_ref, bf16[64,4,32,128]{3,2,1,0:T(8,128)(2,1)S(1)} %all_to_all.15.x_ref, bf16[8,128,128]{2,1,0:T(8,128)(2,1)S(1)} %all-to-all-done.1.got_ref, f32[2048,128]{1,0:T(8,128)S(1)} %get-tuple-element.6.dq_ref, f32[2048,128]{1,0:T(8,128)} %get-tuple-element.7.refs_0_, ...), custom_call_target="tpu_custom_call" | custom-call | tf_op jit(solution)/shard_map/far/pallas_call | solution.py:239
  75.9 32.1 %all_to_all.16.x_ref = bf16[64,3,32,128]{3,2,1,0:T(8,128)(2,1)S(1)} all-to-all(bf16[64,3,32,128]{3,2,1,0:T(8,128)(2,1)S(1)} %far.1), channel_id=1, replica_groups=mesh['seq'=64,'head'=8] {'seq':(8)8,'head'}, dimensions={0} | all-to-all | bytes 3145728 | tf_op jit(solution)/shard_map/all_to_all | solution.py:258
  108.1 1.3 %unpack.1 = (bf16[32,8192]{1,0:T(8,128)(2,1)}, bf16[32,8192]{1,0:T(8,128)(2,1)}, bf16[32,8192]{1,0:T(8,128)(2,1)}) custom-call(bf16[64,3,32,128]{3,2,1,0:T(8,128)(2,1)S(1)} %all_to_all.16.x_ref), custom_call_target="tpu_custom_call" | custom-call | tf_op jit(solution)/shard_map/unpack/pallas_call | solution.py:112
Async XLA Ops:
  43.5 30.2 %all-to-all-start.1 = ((bf16[8,128,128]{2,1,0:T(8,128)(2,1)}), bf16[8,128,128]{2,1,0:T(8,128)(2,1)S(1)}, u32[]{:S(2)}, u32[]{:S(2)}) async-start(bf16[8,128,128]{2,1,0:T(8,128)(2,1)} %sums.1), calls=%async_computation.1 | async-start | bytes 524288 | tf_op jit(solution)/shard_map/all_to_all | solution.py:258

commit v4 on v3

--- a/solution.py
+++ b/solution.py
@@ -9,6 +9,7 @@
 ROWS = 32
 CHUNK = 256
 STEP = CHUNK // ROWS
+PARTS = 2
 PIECES = 4
 BLOCKS = "block"
 GROUP = "group"
@@ -216,19 +217,24 @@
         at = slice(n * HEAD_DIM, (n + 1) * HEAD_DIM)
         dq_state[:, at] = b
         dk_state[:, at] = s
-        dv_state[at, :] = s
-
-    def add(out, source, near, state, axis):
-        y = rows_of(x_ref, source)
+        dv_state[:, at] = s.T
+
+    rows = held.shape[1] // PARTS
+
+    def add(p, out, source, near, state):
+        y = x_ref[p * (rows // ROWS) : (p + 1) * (rows // ROWS), source].reshape(rows, HEAD_DIM)
         y = jnp.concatenate([y, y], axis=1)
-        value = near[...] + dot(y, state[...], 1, axis)
-        o_ref[:, out] = value.astype(BF16).reshape(-1, ROWS, HEAD_DIM)
-
-    add(0, 2, dq_ref, dq_state, 1)
+        value = near[p * rows : (p + 1) * rows] + dot(y, state[...], 1, 1)
+        o_ref[p * (rows // ROWS) : (p + 1) * (rows // ROWS), out] = value.astype(BF16).reshape(-1, ROWS, HEAD_DIM)
+
+    for p in range(PARTS):
+        add(p, 0, 2, dq_ref, dq_state)
     for a in range(2):
         fetch(a).wait()
-    add(1, 1, held.at[0], dk_state, 1)
-    add(2, 0, held.at[1], dv_state, 0)
+    for p in range(PARTS):
+        add(p, 1, 1, held.at[0], dk_state)
+    for p in range(PARTS):
+        add(p, 2, 0, held.at[1], dv_state)
 
 
 def far(me, x, got, dq, *parts):
@@ -246,7 +252,7 @@
             pltpu.VMEM((2, heads * ROWS, HEAD_DIM), F32),
             wide,
             wide,
-            pltpu.VMEM((2 * HEAD_DIM, HEAD_DIM), BF16),
+            wide,
             pltpu.SemaphoreType.DMA((2,)),
         ],
         compiler_params=params(),

time: 110 us -> 110 us (level)
  no operation moved by 1% of the time
where the time goes in v4:
time: 110 us
  blocking collectives  71 us (65%)
  Pallas kernels  13.4 us (12%)
  starting transfers between devices  13.1 us (12%)
  waiting for transfers between devices  11.4 us (10%)
    all_to_all x2, blocking collectives, swap(): return lax.all_to_all(x, axis, split_axis=0, concat_axis=0, tiled=True)  71 us
    all_to_all x1, starting transfers between devices, swap(): return lax.all_to_all(x, axis, split_axis=0, concat_axis=0, tiled=True)  13.1 us
    all_to_all x1, waiting for transfers between devices, swap(): return lax.all_to_all(x, axis, split_axis=0, concat_axis=0, tiled=True)  11.4 us
    pallas_call x1, Pallas kernels, near(): pl.pallas_call(near_kernel, grid=(chunks,), in_specs=[pl.BlockSpec(memory...  5.62 us
    pallas_call x1, Pallas kernels, pack(): pl.pallas_call(pack_kernel, in_specs=[pl.BlockSpec(memory_space=pltpu.SME...  2.72 us
    pallas_call x1, Pallas kernels, far(): pl.pallas_call(far_kernel, in_specs=[pl.BlockSpec(memory_space=pltpu.SMEM...  2.61 us
  transfers between devices with their start and end apart: 1, of which 1 were waited for; matrix products, arithmetic and copies ran while one was open for 0% of the time, Pallas kernels for 5%

profile of v4, /device:TPU:1, one launch (start us, length us, event | category | flops | bytes accessed | tf_op | source)
XLA Modules:
  0.0 109.6 jit_solution(13370972030003319850)
XLA Ops:
  0.6 2.7 %pack.1 = bf16[64,4,32,128]{3,2,1,0:T(8,128)(2,1)} custom-call(s32[1]{0:T(128)} %bitcast.1.first_ref, bf16[32,8192]{1,0:T(8,128)(2,1)} %refs_0_.1, bf16[32,8192]{1,0:T(8,128)(2,1)} %refs_1_.1, bf16[32,8192]{1,0:T(8,128)(2,1)} %refs_2_.1, bf16[32,8192]{1,0:T(8,128)(2,1)} %refs_3_.1), custom_call_target="tpu_custom_call" | custom-call | tf_op jit(solution)/shard_map/pack/pallas_call | solution.py:73
  3.4 38.9 %all_to_all.15.x_ref = bf16[64,4,32,128]{3,2,1,0:T(8,128)(2,1)S(1)} all-to-all(bf16[64,4,32,128]{3,2,1,0:T(8,128)(2,1)} %pack.1), channel_id=1, replica_groups=mesh['seq'=64,'head'=8] {'seq':(8)8,'head'}, dimensions={0} | all-to-all | bytes 4194304 | tf_op jit(solution)/shard_map/all_to_all | solution.py:264
  42.3 1.2 %sums.1 = bf16[8,128,128]{2,1,0:T(8,128)(2,1)} custom-call(s32[1]{0:T(128)} %bitcast.me_ref, bf16[64,4,32,128]{3,2,1,0:T(8,128)(2,1)S(1)} %all_to_all.15.x_ref), custom_call_target="tpu_custom_call" | custom-call | tf_op jit(solution)/shard_map/sums/pallas_call | solution.py:140
  43.5 13.1 %all-to-all-start.1 = ((bf16[8,128,128]{2,1,0:T(8,128)(2,1)}), bf16[8,128,128]{2,1,0:T(8,128)(2,1)S(1)}, u32[]{:S(2)}, u32[]{:S(2)}) async-start(bf16[8,128,128]{2,1,0:T(8,128)(2,1)} %sums.1), calls=%async_computation.1 | async-start | bytes 524288 | tf_op jit(solution)/shard_map/all_to_all | solution.py:264
  56.6 5.6 %near.1 = (f32[2048,128]{1,0:T(8,128)S(1)}, f32[2048,128]{1,0:T(8,128)}, f32[2048,128]{1,0:T(8,128)}) custom-call(bf16[64,4,32,128]{3,2,1,0:T(8,128)(2,1)S(1)} %all_to_all.15.x_ref), custom_call_target="tpu_custom_call" | custom-call | flops 3000000000 | bytes 8388608 | tf_op jit(solution)/shard_map/near/pallas_call | solution.py:184
  62.2 11.4 %all-to-all-done.1.got_ref = bf16[8,128,128]{2,1,0:T(8,128)(2,1)S(1)} async-done(((bf16[8,128,128]{2,1,0:T(8,128)(2,1)}), bf16[8,128,128]{2,1,0:T(8,128)(2,1)S(1)}, u32[]{:S(2)}, u32[]{:S(2)}) %all-to-all-start.1) | async-done | bytes 262176 | tf_op jit(solution)/shard_map/all_to_all | solution.py:264
  73.6 2.6 %far.1 = bf16[64,3,32,128]{3,2,1,0:T(8,128)(2,1)S(1)} custom-call(s32[1]{0:T(128)} %bitcast.me_ref, bf16[64,4,32,128]{3,2,1,0:T(8,128)(2,1)S(1)} %all_to_all.15.x_ref, bf16[8,128,128]{2,1,0:T(8,128)(2,1)S(1)} %all-to-all-done.1.got_ref, f32[2048,128]{1,0:T(8,128)S(1)} %get-tuple-element.6.dq_ref, f32[2048,128]{1,0:T(8,128)} %get-tuple-element.7.refs_0_, ...), custom_call_target="tpu_custom_call" | custom-call | tf_op jit(solution)/shard_map/far/pallas_call | solution.py:245
  76.3 32.1 %all_to_all.16.x_ref = bf16[64,3,32,128]{3,2,1,0:T(8,128)(2,1)S(1)} all-to-all(bf16[64,3,32,128]{3,2,1,0:T(8,128)(2,1)S(1)} %far.1), channel_id=1, replica_groups=mesh['seq'=64,'head'=8] {'seq':(8)8,'head'}, dimensions={0} | all-to-all | bytes 3145728 | tf_op jit(solution)/shard_map/all_to_all | solution.py:264
  108.4 1.3 %unpack.1 = (bf16[32,8192]{1,0:T(8,128)(2,1)}, bf16[32,8192]{1,0:T(8,128)(2,1)}, bf16[32,8192]{1,0:T(8,128)(2,1)}) custom-call(bf16[64,3,32,128]{3,2,1,0:T(8,128)(2,1)S(1)} %all_to_all.16.x_ref), custom_call_target="tpu_custom_call" | custom-call | tf_op jit(solution)/shard_map/unpack/pallas_call | solution.py:113
Async XLA Ops:
  43.5 30.2 %all-to-all-start.1 = ((bf16[8,128,128]{2,1,0:T(8,128)(2,1)}), bf16[8,128,128]{2,1,0:T(8,128)(2,1)S(1)}, u32[]{:S(2)}, u32[]{:S(2)}) async-start(bf16[8,128,128]{2,1,0:T(8,128)(2,1)} %sums.1), calls=%async_computation.1 | async-start | bytes 524288 | tf_op jit(solution)/shard_map/all_to_all | solution.py:264

commit v5 on v3

--- a/solution.py
+++ b/solution.py
@@ -9,7 +9,7 @@
 ROWS = 32
 CHUNK = 256
 STEP = CHUNK // ROWS
-PIECES = 4
+PIECES = 2
 BLOCKS = "block"
 GROUP = "group"
 AXES = (BLOCKS, GROUP)

time: 110 us -> 110 us (level)
  no operation moved by 1% of the time
where the time goes in v5:
time: 110 us; the launch traced here: 109 us
  blocking collectives  71.1 us (65%)
  Pallas kernels  13.1 us (12%)
  starting transfers between devices  13.1 us (12%)
  waiting for transfers between devices  11.4 us (10%)
    all_to_all x2, blocking collectives, swap(): return lax.all_to_all(x, axis, split_axis=0, concat_axis=0, tiled=True)  71.1 us
    all_to_all x1, starting transfers between devices, swap(): return lax.all_to_all(x, axis, split_axis=0, concat_axis=0, tiled=True)  13.1 us
    all_to_all x1, waiting for transfers between devices, swap(): return lax.all_to_all(x, axis, split_axis=0, concat_axis=0, tiled=True)  11.4 us
    pallas_call x1, Pallas kernels, near(): pl.pallas_call(near_kernel, grid=(chunks,), in_specs=[pl.BlockSpec(memory...  5.62 us
    pallas_call x1, Pallas kernels, pack(): pl.pallas_call(pack_kernel, in_specs=[pl.BlockSpec(memory_space=pltpu.SME...  2.76 us
    pallas_call x1, Pallas kernels, far(): pl.pallas_call(far_kernel, in_specs=[pl.BlockSpec(memory_space=pltpu.SMEM...  2.28 us
  transfers between devices with their start and end apart: 1, of which 1 were waited for; matrix products, arithmetic and copies ran while one was open for 0% of the time, Pallas kernels for 5%

profile of v5, /device:TPU:1, one launch (start us, length us, event | category | flops | bytes accessed | tf_op | source)
XLA Modules:
  0.0 109.3 jit_solution(3395992096520519346)
XLA Ops:
  0.6 2.8 %pack.1 = bf16[64,4,32,128]{3,2,1,0:T(8,128)(2,1)} custom-call(s32[1]{0:T(128)} %bitcast.1.first_ref, bf16[32,8192]{1,0:T(8,128)(2,1)} %refs_0_.1, bf16[32,8192]{1,0:T(8,128)(2,1)} %refs_1_.1, bf16[32,8192]{1,0:T(8,128)(2,1)} %refs_2_.1, bf16[32,8192]{1,0:T(8,128)(2,1)} %refs_3_.1), custom_call_target="tpu_custom_call" | custom-call | tf_op jit(solution)/shard_map/pack/pallas_call | solution.py:72
  3.4 38.9 %all_to_all.15.x_ref = bf16[64,4,32,128]{3,2,1,0:T(8,128)(2,1)S(1)} all-to-all(bf16[64,4,32,128]{3,2,1,0:T(8,128)(2,1)} %pack.1), channel_id=1, replica_groups=mesh['seq'=64,'head'=8] {'seq':(8)8,'head'}, dimensions={0} | all-to-all | bytes 4194304 | tf_op jit(solution)/shard_map/all_to_all | solution.py:258
  42.3 1.2 %sums.1 = bf16[8,128,128]{2,1,0:T(8,128)(2,1)} custom-call(s32[1]{0:T(128)} %bitcast.me_ref, bf16[64,4,32,128]{3,2,1,0:T(8,128)(2,1)S(1)} %all_to_all.15.x_ref), custom_call_target="tpu_custom_call" | custom-call | tf_op jit(solution)/shard_map/sums/pallas_call | solution.py:139
  43.5 13.1 %all-to-all-start.1 = ((bf16[8,128,128]{2,1,0:T(8,128)(2,1)}), bf16[8,128,128]{2,1,0:T(8,128)(2,1)S(1)}, u32[]{:S(2)}, u32[]{:S(2)}) async-start(bf16[8,128,128]{2,1,0:T(8,128)(2,1)} %sums.1), calls=%async_computation.1 | async-start | bytes 524288 | tf_op jit(solution)/shard_map/all_to_all | solution.py:258
  56.6 5.6 %near.1 = (f32[2048,128]{1,0:T(8,128)S(1)}, f32[2048,128]{1,0:T(8,128)}, f32[2048,128]{1,0:T(8,128)}) custom-call(bf16[64,4,32,128]{3,2,1,0:T(8,128)(2,1)S(1)} %all_to_all.15.x_ref), custom_call_target="tpu_custom_call" | custom-call | flops 3000000000 | bytes 8388608 | tf_op jit(solution)/shard_map/near/pallas_call | solution.py:183
  62.2 11.4 %all-to-all-done.1.got_ref = bf16[8,128,128]{2,1,0:T(8,128)(2,1)S(1)} async-done(((bf16[8,128,128]{2,1,0:T(8,128)(2,1)}), bf16[8,128,128]{2,1,0:T(8,128)(2,1)S(1)}, u32[]{:S(2)}, u32[]{:S(2)}) %all-to-all-start.1) | async-done | bytes 262176 | tf_op jit(solution)/shard_map/all_to_all | solution.py:258
  73.7 2.3 %far.1 = bf16[64,3,32,128]{3,2,1,0:T(8,128)(2,1)S(1)} custom-call(s32[1]{0:T(128)} %bitcast.me_ref, bf16[64,4,32,128]{3,2,1,0:T(8,128)(2,1)S(1)} %all_to_all.15.x_ref, bf16[8,128,128]{2,1,0:T(8,128)(2,1)S(1)} %all-to-all-done.1.got_ref, f32[2048,128]{1,0:T(8,128)S(1)} %get-tuple-element.6.dq_ref, f32[2048,128]{1,0:T(8,128)} %get-tuple-element.7.refs_0_, ...), custom_call_target="tpu_custom_call" | custom-call | tf_op jit(solution)/shard_map/far/pallas_call | solution.py:239
  76.0 32.1 %all_to_all.16.x_ref = bf16[64,3,32,128]{3,2,1,0:T(8,128)(2,1)S(1)} all-to-all(bf16[64,3,32,128]{3,2,1,0:T(8,128)(2,1)S(1)} %far.1), channel_id=1, replica_groups=mesh['seq'=64,'head'=8] {'seq':(8)8,'head'}, dimensions={0} | all-to-all | bytes 3145728 | tf_op jit(solution)/shard_map/all_to_all | solution.py:258
  108.1 1.2 %unpack.1 = (bf16[32,8192]{1,0:T(8,128)(2,1)}, bf16[32,8192]{1,0:T(8,128)(2,1)}, bf16[32,8192]{1,0:T(8,128)(2,1)}) custom-call(bf16[64,3,32,128]{3,2,1,0:T(8,128)(2,1)S(1)} %all_to_all.16.x_ref), custom_call_target="tpu_custom_call" | custom-call | tf_op jit(solution)/shard_map/unpack/pallas_call | solution.py:112
Async XLA Ops:
  43.5 30.2 %all-to-all-start.1 = ((bf16[8,128,128]{2,1,0:T(8,128)(2,1)}), bf16[8,128,128]{2,1,0:T(8,128)(2,1)S(1)}, u32[]{:S(2)}, u32[]{:S(2)}) async-start(bf16[8,128,128]{2,1,0:T(8,128)(2,1)} %sums.1), calls=%async_computation.1 | async-start | bytes 524288 | tf_op jit(solution)/shard_map/all_to_all | solution.py:258

commit v6 on v3

--- a/solution.py
+++ b/solution.py
@@ -9,6 +9,7 @@
 ROWS = 32
 CHUNK = 256
 STEP = CHUNK // ROWS
+TILE = 8
 PIECES = 4
 BLOCKS = "block"
 GROUP = "group"
@@ -87,40 +88,37 @@
 
 
 def unpack_kernel(x_ref, *refs):
-    outs, (made, sem) = refs[:3], refs[3:]
-    width = made.shape[2]
-    columns = width // PIECES
-    heads = columns // HEAD_DIM
-
-    def send(p, a):
-        at = (slice(None), pl.ds(p * columns, columns))
-        return pltpu.make_async_copy(made.at[(a, *at)], outs[a].at[at], sem.at[p, a])
-
-    for p in range(PIECES):
-        for a in range(3):
-            for h in range(p * heads, (p + 1) * heads):
-                made[a, :, h * HEAD_DIM : (h + 1) * HEAD_DIM] = x_ref[h, a]
-            send(p, a).start()
-    for p in range(PIECES):
-        for a in range(3):
-            send(p, a).wait()
+    outs, sem = refs[:3], refs[3]
+
+    def move(a, r):
+        here = x_ref.at[:, a, pl.ds(r * TILE, TILE)]
+        return pltpu.make_async_copy(here, outs[a].at[r], sem.at[a, r])
+
+    for a in range(3):
+        for r in range(ROWS // TILE):
+            move(a, r).start()
+    for a in range(3):
+        for r in range(ROWS // TILE):
+            move(a, r).wait()
+
+
+def untiled(x):
+    n, heads, _, _ = x.shape
+    return jnp.transpose(x, (0, 2, 1, 3)).reshape(n * TILE, heads * HEAD_DIM)
 
 
 def unpack(x):
     heads, n, rows, _ = x.shape
-    width = heads * HEAD_DIM
-    return pl.pallas_call(
+    outs = pl.pallas_call(
         unpack_kernel,
         in_specs=[pl.BlockSpec(memory_space=pltpu.VMEM)],
         out_specs=[pl.BlockSpec(memory_space=pltpu.HBM)] * n,
-        out_shape=[pltpu.HBM((rows, width), x.dtype)] * n,
-        scratch_shapes=[
-            pltpu.VMEM((n, rows, width), x.dtype),
-            pltpu.SemaphoreType.DMA((PIECES, n)),
-        ],
+        out_shape=[pltpu.HBM((rows // TILE, heads, TILE, HEAD_DIM), x.dtype)] * n,
+        scratch_shapes=[pltpu.SemaphoreType.DMA((n, rows // TILE))],
         compiler_params=params(),
         name="unpack",
     )(x)
+    return [untiled(y) for y in outs]
 
 
 def rows_of(x_ref, a, c=None):

time: 110 us -> 110 us (level)
  no operation moved by 1% of the time
where the time goes in v6:
time: 110 us; the launch traced here: 109 us
  blocking collectives  71.1 us (65%)
  starting transfers between devices  13.1 us (12%)
  Pallas kernels  13 us (12%)
  waiting for transfers between devices  11.4 us (10%)
    all_to_all x2, blocking collectives, swap(): return lax.all_to_all(x, axis, split_axis=0, concat_axis=0, tiled=True)  71.1 us
    all_to_all x1, starting transfers between devices, swap(): return lax.all_to_all(x, axis, split_axis=0, concat_axis=0, tiled=True)  13.1 us
    all_to_all x1, waiting for transfers between devices, swap(): return lax.all_to_all(x, axis, split_axis=0, concat_axis=0, tiled=True)  11.4 us
    pallas_call x1, Pallas kernels, near(): pl.pallas_call(near_kernel, grid=(chunks,), in_specs=[pl.BlockSpec(memory...  5.62 us
    pallas_call x1, Pallas kernels, pack(): pl.pallas_call(pack_kernel, in_specs=[pl.BlockSpec(memory_space=pltpu.SME...  2.71 us
    pallas_call x1, Pallas kernels, far(): pl.pallas_call(far_kernel, in_specs=[pl.BlockSpec(memory_space=pltpu.SMEM...  2.27 us
  transfers between devices with their start and end apart: 1, of which 1 were waited for; matrix products, arithmetic and copies ran while one was open for 0% of the time, Pallas kernels for 5%

profile of v6, /device:TPU:1, one launch (start us, length us, event | category | flops | bytes accessed | tf_op | source)
XLA Modules:
  0.0 109.3 jit_solution(8869538567206210573)
XLA Ops:
  0.6 2.7 %pack.1 = bf16[64,4,32,128]{3,2,1,0:T(8,128)(2,1)} custom-call(s32[1]{0:T(128)} %bitcast.1.first_ref, bf16[32,8192]{1,0:T(8,128)(2,1)} %refs_0_.1, bf16[32,8192]{1,0:T(8,128)(2,1)} %refs_1_.1, bf16[32,8192]{1,0:T(8,128)(2,1)} %refs_2_.1, bf16[32,8192]{1,0:T(8,128)(2,1)} %refs_3_.1), custom_call_target="tpu_custom_call" | custom-call | tf_op jit(solution)/shard_map/pack/pallas_call | solution.py:73
  3.4 38.9 %all_to_all.15.x_ref = bf16[64,4,32,128]{3,2,1,0:T(8,128)(2,1)S(1)} all-to-all(bf16[64,4,32,128]{3,2,1,0:T(8,128)(2,1)} %pack.1), channel_id=1, replica_groups=mesh['seq'=64,'head'=8] {'seq':(8)8,'head'}, dimensions={0} | all-to-all | bytes 4194304 | tf_op jit(solution)/shard_map/all_to_all | solution.py:256
  42.3 1.2 %sums.1 = bf16[8,128,128]{2,1,0:T(8,128)(2,1)} custom-call(s32[1]{0:T(128)} %bitcast.me_ref, bf16[64,4,32,128]{3,2,1,0:T(8,128)(2,1)S(1)} %all_to_all.15.x_ref), custom_call_target="tpu_custom_call" | custom-call | tf_op jit(solution)/shard_map/sums/pallas_call | solution.py:137
  43.5 13.1 %all-to-all-start.1 = ((bf16[8,128,128]{2,1,0:T(8,128)(2,1)}), bf16[8,128,128]{2,1,0:T(8,128)(2,1)S(1)}, u32[]{:S(2)}, u32[]{:S(2)}) async-start(bf16[8,128,128]{2,1,0:T(8,128)(2,1)} %sums.1), calls=%async_computation.1 | async-start | bytes 524288 | tf_op jit(solution)/shard_map/all_to_all | solution.py:256
  56.6 5.6 %near.1 = (f32[2048,128]{1,0:T(8,128)S(1)}, f32[2048,128]{1,0:T(8,128)}, f32[2048,128]{1,0:T(8,128)}) custom-call(bf16[64,4,32,128]{3,2,1,0:T(8,128)(2,1)S(1)} %all_to_all.15.x_ref), custom_call_target="tpu_custom_call" | custom-call | flops 3000000000 | bytes 8388608 | tf_op jit(solution)/shard_map/near/pallas_call | solution.py:181
  62.2 11.4 %all-to-all-done.1.got_ref = bf16[8,128,128]{2,1,0:T(8,128)(2,1)S(1)} async-done(((bf16[8,128,128]{2,1,0:T(8,128)(2,1)}), bf16[8,128,128]{2,1,0:T(8,128)(2,1)S(1)}, u32[]{:S(2)}, u32[]{:S(2)}) %all-to-all-start.1) | async-done | bytes 262176 | tf_op jit(solution)/shard_map/all_to_all | solution.py:256
  73.6 2.3 %far.1 = bf16[64,3,32,128]{3,2,1,0:T(8,128)(2,1)S(1)} custom-call(s32[1]{0:T(128)} %bitcast.me_ref, bf16[64,4,32,128]{3,2,1,0:T(8,128)(2,1)S(1)} %all_to_all.15.x_ref, bf16[8,128,128]{2,1,0:T(8,128)(2,1)S(1)} %all-to-all-done.1.got_ref, f32[2048,128]{1,0:T(8,128)S(1)} %get-tuple-element.9.dq_ref, f32[2048,128]{1,0:T(8,128)} %get-tuple-element.10.refs_0_, ...), custom_call_target="tpu_custom_call" | custom-call | tf_op jit(solution)/shard_map/far/pallas_call | solution.py:237
  75.9 32.1 %all_to_all.16.x_ref = bf16[64,3,32,128]{3,2,1,0:T(8,128)(2,1)S(1)} all-to-all(bf16[64,3,32,128]{3,2,1,0:T(8,128)(2,1)S(1)} %far.1), channel_id=1, replica_groups=mesh['seq'=64,'head'=8] {'seq':(8)8,'head'}, dimensions={0} | all-to-all | bytes 3145728 | tf_op jit(solution)/shard_map/all_to_all | solution.py:256
  108.1 1.2 %unpack.1 = (bf16[4,64,8,128]{3,2,1,0:T(8,128)(2,1)}, bf16[4,64,8,128]{3,2,1,0:T(8,128)(2,1)}, bf16[4,64,8,128]{3,2,1,0:T(8,128)(2,1)}) custom-call(bf16[64,3,32,128]{3,2,1,0:T(8,128)(2,1)S(1)} %all_to_all.16.x_ref), custom_call_target="tpu_custom_call" | custom-call | tf_op jit(solution)/shard_map/unpack/pallas_call | solution.py:112
Async XLA Ops:
  43.5 30.2 %all-to-all-start.1 = ((bf16[8,128,128]{2,1,0:T(8,128)(2,1)}), bf16[8,128,128]{2,1,0:T(8,128)(2,1)S(1)}, u32[]{:S(2)}, u32[]{:S(2)}) async-start(bf16[8,128,128]{2,1,0:T(8,128)(2,1)} %sums.1), calls=%async_computation.1 | async-start | bytes 524288 | tf_op jit(solution)/shard_map/all_to_all | solution.py:256
